TPU v7x, 256 devices: a whole 4x4x8 slice. The times are simulated.
256 devices in a mesh: tracer: 8 (over y, x_lo), gx: 4 (over x_hi, core), gy: 8 (over z).
Axes of the slice: x: 4 (x_hi: 2, x_lo: 2; x = x_hi * 2 + x_lo), y: 4, z: 8, core: 2. Of those that a mesh axis runs over, the one named last changes fastest.
Arguments:
- tracers: float32 [96, 16, 32, 1024], P('tracer', None, 'gx', 'gy'), may hold values from 0.05 to 2
- fluxes: float32 [3, 16, 32, 1024], P(None, 'tracer', 'gx', 'gy'), may hold values from -0.15 to 0.15
- diff_east: float32 [32, 1024], P('gx', 'gy'), may hold values from 0.01 to 0.1
- diff_north: float32 [32, 1024], P('gx', 'gy'), may hold values from 0.01 to 0.1
- column_depth: int32 [32, 1024], P('gx', 'gy'), may hold values from 0 to 16
- grazers: float32 [16, 32, 1024], P(None, 'gx', 'gy'), may hold values from 0.2 to 0.9
- groups: int32 [96], P('tracer'), may hold values from 0 to 15
- preference: float32 [16], replicated, may hold values from 0.1 to 1
Outputs:
- advanced: float32 [96, 16, 32, 1024], P('tracer', None, 'gx', 'gy')
Inputs may be any that keep to these rules, and one draw needn't show every extreme that they name: A cell at level k is sea iff k < column_depth of its column.
All inputs are finite; a program needn't handle non-finite values.
Results may differ from a plain program's by a relative error of at most 0.0003.
Values sent between devices are 32-bit elements; how exact they have to be, the bound alone decides.
A program may use at most 64 MiB of HBM per device.

v0:
```python
import jax
import jax.numpy as jnp
from jax import lax
from jax.sharding import PartitionSpec as P

STEPS = 2


def in_order(pieces, dim):
    pieces = jnp.moveaxis(pieces, 0, dim)
    lengths = pieces.shape
    return pieces.reshape(*lengths[:dim], lengths[dim] * lengths[dim + 1], *lengths[dim + 2 :])


def from_everyone(shard, axis):
    copies = jnp.broadcast_to(shard, (lax.axis_size(axis), *shard.shape))
    return lax.all_to_all(copies, axis, split_axis=0, concat_axis=0, tiled=True)


def gathered_copies(shard, axis, dim):
    return in_order(from_everyone(shard, axis), dim)


def with_halo(shard, sides, width):
    edges = {}
    for axis, dim in sides:
        size, length = (lax.axis_size(axis), shard.shape[dim])
        up = [(i, (i + 1) % size) for i in range(size - 1)]
        last = lax.slice_in_dim(shard, length - width, length, axis=dim)
        initial = lax.slice_in_dim(shard, 0, width, axis=dim)
        edges[dim] = (
            lax.ppermute(last, axis, up),
            lax.ppermute(initial, axis, [(b, a) for a, b in up]),
        )
    done = []
    for _, dim in sides:
        low, high = edges[dim]
        around = [(width, width) if d in done else (0, 0) for d in range(shard.ndim)]
        shard = jnp.concatenate([jnp.pad(low, around), shard, jnp.pad(high, around)], axis=dim)
        done.append(dim)
    return shard


def of_everyone(shard, axis):
    everything = from_everyone(shard, axis)
    return jnp.sum(everything, axis=0)


def minmod(jump_low, jump_high):
    return jnp.maximum(0.0, jnp.minimum(jump_low, jump_high)) + jnp.minimum(
        0.0, jnp.maximum(jump_low, jump_high)
    )


def window(values, low_end, high_end, direction):
    return lax.slice_in_dim(values, low_end, high_end, axis=direction % values.ndim)


def face_terms(tracer_field, open_faces, face_flux, face_kappa, direction):
    length = tracer_field.shape[direction % tracer_field.ndim] - 4
    jump_face = open_faces * (
        window(tracer_field, 1, length + 4, direction)
        - window(tracer_field, 0, length + 3, direction)
    )
    slopes = minmod(
        window(jump_face, 0, length + 2, direction), window(jump_face, 1, length + 3, direction)
    )
    left_value = window(tracer_field, 1, length + 2, direction) + 0.5 * window(
        slopes, 0, length + 1, direction
    )
    right_value = window(tracer_field, 2, length + 3, direction) - 0.5 * window(
        slopes, 1, length + 2, direction
    )
    carried = face_flux * jnp.where(face_flux > 0.0, left_value, right_value)
    if face_kappa is not None:
        carried = carried - face_kappa * window(jump_face, 1, length + 2, direction)
    return window(carried, 0, length, direction) - window(carried, 1, length + 1, direction)


def on_device(tracers, fluxes, diff_east, diff_north, column_depth, grazers, groups, preference):
    tr_dev, levels, rows_dev, cols_dev = tracers.shape
    total_tracers = tr_dev * lax.axis_size("tracer")
    level_index = lax.broadcasted_iota(jnp.int32, (levels, rows_dev, cols_dev), 0)
    wet_cells = (level_index < column_depth[None]).astype(jnp.float32)
    all_fluxes = gathered_copies(fluxes, "tracer", 1)
    stacked = jnp.concatenate(
        [all_fluxes[0], all_fluxes[1], wet_cells, diff_east[None], diff_north[None]], 0
    )
    rimmed = with_halo(stacked, (("gx", 1), ("gy", 2)), 2)
    east_ext = rimmed[:levels]
    north_ext = rimmed[levels : 2 * levels]
    downward = all_fluxes[2]
    wet_ext = rimmed[-(levels + 2) : -2]
    kx_ext = rimmed[-2]
    ky_ext = rimmed[-1]
    open_x = wet_ext[:, :-1, 2:-2] * wet_ext[:, 1:, 2:-2]
    open_y = wet_ext[:, 2:-2, :-1] * wet_ext[:, 2:-2, 1:]
    flux_x = east_ext[:, 1 : rows_dev + 2, 2:-2] * open_x[:, 1 : rows_dev + 2]
    kappa_x = kx_ext[None, 1 : rows_dev + 2, 2:-2] * open_x[:, 1 : rows_dev + 2]
    flux_y = north_ext[:, 2:-2, 1 : cols_dev + 2] * open_y[:, :, 1 : cols_dev + 2]
    kappa_y = ky_ext[None, 2:-2, 1 : cols_dev + 2] * open_y[:, :, 1 : cols_dev + 2]
    wet_z = jnp.pad(wet_cells, ((2, 2), (0, 0), (0, 0)))
    open_z = wet_z[:-1] * wet_z[1:]
    flux_z = jnp.pad(downward, ((1, 0), (0, 0), (0, 0))) * open_z[1 : levels + 2]
    group_match = (
        groups[:, None] == lax.broadcasted_iota(jnp.int32, (1, preference.shape[0]), 1)
    ).astype(jnp.float32)
    grazing_pref = jnp.sum(group_match * preference[None, :], axis=1)
    tracer_field = tracers
    for step_index in range(STEPS):
        prey_local = jnp.sum(grazing_pref[:, None, None, None] * tracer_field, axis=0)
        prey_total = of_everyone(prey_local, "tracer")
        factor = grazers / (1.0 + 4.0 * prey_total / total_tracers)
        extended = with_halo(tracer_field, (("gx", 2), ("gy", 3)), 2)
        tendency = face_terms(extended[:, :, :, 2:-2], open_x, flux_x, kappa_x, -2)
        tendency = tendency + face_terms(extended[:, :, 2:-2, :], open_y, flux_y, kappa_y, -1)
        padded_z = jnp.pad(tracer_field, ((0, 0), (2, 2), (0, 0), (0, 0)))
        tendency = tendency + face_terms(padded_z, open_z, flux_z, None, -3)
        tracer_field = (
            tracer_field + tendency - grazing_pref[:, None, None, None] * factor * tracer_field
        )
    return tracer_field


def solution(mesh):
    placed = (
        P("tracer", None, "gx", "gy"),
        P(None, "tracer", "gx", "gy"),
        P("gx", "gy"),
        P("gx", "gy"),
        P("gx", "gy"),
        P(None, "gx", "gy"),
        P("tracer"),
        P(),
    )
    return jax.shard_map(
        on_device,
        mesh=mesh,
        in_specs=placed,
        out_specs=P("tracer", None, "gx", "gy"),
        check_vma=False,
    )
```

profile of v0, /device:TPU:134, one launch (start us, length us, event | category | flops | bytes accessed | tf_op | source)
XLA Modules:
  0.0 128.5 jit_solution(11300637712447472433)
XLA Ops:
  1.4 5.9 %all-to-all-start = ((f32[8,3,2,8,128]{4,3,2,1,0:T(8,128)}), f32[8,3,2,8,128]{4,3,2,1,0:T(8,128)S(1)}, u32[]{:S(2)}, u32[]{:S(2)}) async-start(f32[8,3,2,8,128]{4,3,2,1,0:T(8,128)} %broadcast_in_dim.25), calls=%async_computation | async-start | bytes 393216 | tf_op jit(solution)/shard_map/all_to_all | solution.py:17
  11.4 5.1 %collective-permute-start.3 = (f32[12,16,2,128]{3,1,2,0:T(8,128)}, f32[12,16,2,128]{3,1,2,0:T(8,128)}, u32[]{:S(2)}, u32[]{:S(2)}) collective-permute-start(f32[12,16,2,128]{3,1,2,0:T(8,128)} %get-tuple-element.19), channel_id=1, source_target_pairs={{8,0},{16,8},{24,16},{9,1},{17,9},{25,17},{10,2},{18,10},{26,18},{... | collective-permute-start | bytes 589832 | tf_op jit(solution)/shard_map/ppermute | solution.py:33
  17.5 2.9 %collective-permute-start.6 = (f32[12,16,8,2]{1,2,3,0:T(8,128)S(1)}, f32[12,16,8,2]{1,2,3,0:T(8,128)}, u32[]{:S(2)}, u32[]{:S(2)}) collective-permute-start(f32[12,16,8,2]{1,2,3,0:T(8,128)S(1)} %copy.141), channel_id=1, source_target_pairs={{0,1},{1,2},{2,3},{3,4},{4,5},{5,6},{6,7},{8,9},{9,10},{10,11},{11... | collective-permute-start | bytes 36872 | tf_op jit(solution)/shard_map/ppermute | solution.py:32
  21.1 4.1 %collective-permute-start.7 = (f32[12,16,8,2]{1,2,3,0:T(8,128)S(1)}, f32[12,16,8,2]{1,2,3,0:T(8,128)S(1)}, u32[]{:S(2)}, u32[]{:S(2)}) collective-permute-start(f32[12,16,8,2]{1,2,3,0:T(8,128)S(1)} %copy.142), channel_id=1, source_target_pairs={{1,0},{2,1},{3,2},{4,3},{5,4},{6,5},{7,6},{9,8},{10,9},{11,10},{12... | collective-permute-start | bytes 36872 | tf_op jit(solution)/shard_map/ppermute | solution.py:33
  26.4 2.4 %copy.143 = f32[12,16,8,2]{3,1,2,0:T(8,128)} copy(f32[12,16,8,2]{1,2,3,0:T(8,128)} %collective-permute-done.6) | data formatting | bytes 24576
  28.8 2.3 %pad.37.clone = f32[12,16,12,2]{3,1,2,0:T(8,128)} pad(f32[12,16,8,2]{3,1,2,0:T(8,128)} %copy.143, f32[]{:T(128)} %constant.6.clone.1), padding=0_0x0_0x2_2x0_0 | pad | bytes 30724 | tf_op jit(solution)/shard_map/jit(_pad)/pad | solution.py:39
  32.6 2.3 %pad.38.clone = f32[12,16,12,2]{3,1,2,0:T(8,128)} pad(f32[12,16,8,2]{3,1,2,0:T(8,128)} %copy.144, f32[]{:T(128)} %constant.6.clone.1), padding=0_0x0_0x2_2x0_0 | pad | bytes 30724 | tf_op jit(solution)/shard_map/jit(_pad)/pad | solution.py:39
  38.4 5.1 %collective-permute-start.1 = (f32[50,2,128]{2,0,1:T(8,128)}, f32[50,2,128]{2,0,1:T(8,128)}, u32[]{:S(2)}, u32[]{:S(2)}) collective-permute-start(f32[50,2,128]{2,0,1:T(8,128)} %get-tuple-element.28), channel_id=1, source_target_pairs={{8,0},{16,8},{24,16},{9,1},{17,9},{25,17},{10,2},{18,10},{26,18},{... | collective-permute-start | bytes 153608 | tf_op jit(solution)/shard_map/ppermute | solution.py:33
  47.0 5.7 %collective-permute-done.4 = f32[50,8,2]{2,0,1:T(8,128)S(1)} collective-permute-done((f32[50,8,2]{2,0,1:T(8,128)S(1)}, f32[50,8,2]{2,0,1:T(8,128)S(1)}, u32[]{:S(2)}, u32[]{:S(2)}) %collective-permute-start.4) | collective-permute-done | bytes 3232 | tf_op jit(solution)/shard_map/ppermute | solution.py:32
  56.6 5.7 %all-to-all-start.1 = ((f32[8,16,8,128]{3,2,1,0:T(8,128)}), f32[8,16,8,128]{3,2,1,0:T(8,128)}, u32[]{:S(2)}, u32[]{:S(2)}) async-start(f32[8,16,8,128]{3,2,1,0:T(8,128)} %broadcast_in_dim.31), calls=%async_computation.1 | async-start | bytes 1048576 | tf_op jit(solution)/shard_map/all_to_all | solution.py:17
  63.3 2.6 %pad_maximum_fusion = f32[12,16,12,132]{3,1,2,0:T(8,128)S(1)} fusion(f32[12,16,12,2]{3,1,2,0:T(8,128)} %pad.38.clone, f32[12,16,12,128]{3,1,2,0:T(8,128)S(1)} %constant_dynamic-update-slice_fusion, f32[12,16,12,2]{3,1,2,0:T(8,128)} %pad.37.clone), kind=kLoop, calls=%fused_computation | loop fusion | flops 608256 | bytes 2433024 | tf_op jit(solution)/shard_map/concatenate | solution.py:39
  70.2 2.3 %fusion.31 = f32[12,16,9,128]{3,1,2,0:T(8,128)} fusion(f32[12,16,11,128]{3,1,2,0:T(8,128)S(1)} %fusion.25, f32[12,16,10,128]{3,1,2,0:T(8,128)S(1)} %minimum_add_fusion.5, f32[12,16,2,128]{3,1,2,0:T(8,128)} %collective-permute-done.3, f32[12,16,8,128]{3,1,2,0:T(8,128)S(1)} %copy.127, f32[12,16,2,128]{3,1,2,0:T(8,128)} %collective-permute-done.2, ...), kind=kLoop, calls=%fused_computation.76 | loop fusion | flops 2211840 | bytes 4884480 | tf_op jit(solution)/shard_map/sub | solution.py:76
  72.7 2.7 %fusion.6 = f32[12,16,8,129]{3,1,2,0:T(8,128)} fusion(f32[12,16,8,131]{3,1,2,0:T(8,128)S(1)} %fusion.11, f32[12,16,8,130]{3,1,2,0:T(8,128)S(1)} %minimum_add_fusion.1, f32[12,16,12,2]{3,1,2,0:T(8,128)S(1)} %copy-done.2, f32[12,16,12,128]{3,1,2,0:T(8,128)S(1)} %constant_dynamic-update-slice_fusion, f32[12,16,12,2]{3,1,2,0:T(8,128)S(1)} %copy-done.1, ...), kind=kLoop, calls=%fused_computation.19 | loop fusion | flops 1981440 | bytes 4535424 | tf_op jit(solution)/shard_map/sub | solution.py:76
  76.7 2.9 %multiply_reduce_fusion = (f32[16,8,128]{2,0,1:T(8,128)S(1)}, f32[12,16,8,128]{3,1,2,0:T(8,128)S(1)}) fusion(f32[12]{0:T(128)S(1)} %select_reduce_fusion, f32[16,8,128]{2,0,1:T(8,128)S(1)} %copy.130, f32[12,17,8,128]{3,1,2,0:T(8,128)} %fusion.14, f32[12,16,8,129]{3,1,2,0:T(8,128)} %fusion.6, f32[12,16,9,128]{3,1,2,0:T(8,128)S(1)} %copy-done.4, ...), kind=kLoop, calls=%fused_computation.99 | loop fusion | flops 2146304 | bytes 6422576 | tf_op jit(solution)/shard_map/reduce_sum | solution.py:111
  83.9 5.1 %collective-permute-start.9 = (f32[12,16,2,128]{3,1,2,0:T(8,128)}, f32[12,16,2,128]{3,1,2,0:T(8,128)S(1)}, u32[]{:S(2)}, u32[]{:S(2)}) collective-permute-start(f32[12,16,2,128]{3,1,2,0:T(8,128)} %get-tuple-element.16), channel_id=1, source_target_pairs={{8,0},{16,8},{24,16},{9,1},{17,9},{25,17},{10,2},{18,10},{26,18},{... | collective-permute-start | bytes 589832 | tf_op jit(solution)/shard_map/ppermute | solution.py:33
  89.0 2.4 %copy.132 = f32[12,16,8,2]{1,2,3,0:T(8,128)} copy(f32[12,16,8,2]{3,1,2,0:T(8,128)} %get-tuple-element.13) | data formatting | bytes 24576 | tf_op jit(solution)/shard_map/slice | solution.py:29
  91.4 3.9 %collective-permute-start.10 = (f32[12,16,8,2]{1,2,3,0:T(8,128)}, f32[12,16,8,2]{1,2,3,0:T(8,128)}, u32[]{:S(2)}, u32[]{:S(2)}) collective-permute-start(f32[12,16,8,2]{1,2,3,0:T(8,128)} %copy.132), channel_id=1, source_target_pairs={{0,1},{1,2},{2,3},{3,4},{4,5},{5,6},{6,7},{8,9},{9,10},{10,11},{11... | collective-permute-start | bytes 36872 | tf_op jit(solution)/shard_map/ppermute | solution.py:32
  95.4 2.4 %copy.134 = f32[12,16,8,2]{1,2,3,0:T(8,128)} copy(f32[12,16,8,2]{3,1,2,0:T(8,128)} %get-tuple-element.14) | data formatting | bytes 24576 | tf_op jit(solution)/shard_map/slice | solution.py:30
  97.8 3.4 %collective-permute-start.11 = (f32[12,16,8,2]{1,2,3,0:T(8,128)}, f32[12,16,8,2]{1,2,3,0:T(8,128)}, u32[]{:S(2)}, u32[]{:S(2)}) collective-permute-start(f32[12,16,8,2]{1,2,3,0:T(8,128)} %copy.134), channel_id=1, source_target_pairs={{1,0},{2,1},{3,2},{4,3},{5,4},{6,5},{7,6},{9,8},{10,9},{11,10},{12... | collective-permute-start | bytes 36872 | tf_op jit(solution)/shard_map/ppermute | solution.py:33
  103.8 5.7 %all-to-all-start.2 = ((f32[8,16,8,128]{3,2,1,0:T(8,128)}), f32[8,16,8,128]{3,2,1,0:T(8,128)S(1)}, u32[]{:S(2)}, u32[]{:S(2)}) async-start(f32[8,16,8,128]{3,2,1,0:T(8,128)} %broadcast_in_dim.32), calls=%async_computation.2 | async-start | bytes 1048576 | tf_op jit(solution)/shard_map/all_to_all | solution.py:17
  109.5 2.4 %copy.133 = f32[12,16,8,2]{3,1,2,0:T(8,128)} copy(f32[12,16,8,2]{1,2,3,0:T(8,128)} %collective-permute-done.10) | data formatting | bytes 24576 | tf_op jit(solution)/shard_map/ppermute | solution.py:32
  113.2 2.4 %copy.135 = f32[12,16,8,2]{3,1,2,0:T(8,128)} copy(f32[12,16,8,2]{1,2,3,0:T(8,128)} %collective-permute-done.11) | data formatting | bytes 24576 | tf_op jit(solution)/shard_map/ppermute | solution.py:33
  120.8 2.7 %fusion = f32[12,16,8,129]{3,1,2,0:T(8,128)} fusion(f32[12,16,8,131]{3,1,2,0:T(8,128)S(1)} %fusion.5, f32[12,16,8,130]{3,1,2,0:T(8,128)S(1)} %minimum_add_fusion, f32[12,16,12,2]{3,1,2,0:T(8,128)S(1)} %pad.43, f32[12,16,2,128]{3,1,2,0:T(8,128)S(1)} %collective-permute-done.9, f32[12,16,8,128]{3,1,2,0:T(8,128)S(1)} %get-tuple-element.6, ...), kind=kLoop, calls=%fused_computation.3 | loop fusion | flops 2774016 | bytes 4535424 | tf_op jit(solution)/shard_map/sub | solution.py:76
  124.7 2.7 %fusion.38 = f32[12,16,8,128]{3,1,2,0:T(8,128)S(1)} fusion(f32[12,16,8,128]{3,1,2,0:T(8,128)S(1)} %get-tuple-element.6, f32[12,17,8,128]{3,1,2,0:T(8,128)} %fusion.20, f32[12,16,8,129]{3,1,2,0:T(8,128)} %fusion, f32[12,16,9,128]{3,1,2,0:T(8,128)S(1)} %copy-done.3, f32[16,8,128]{2,0,1:T(8,128)S(1)} %copy.137, f32[12]{0:T(128)S(1)} %select_reduce_fusion), kind=kLoop, calls=%fused_computation.88 | loop fusion | flops 1769472 | bytes 6357040 | tf_op jit(solution)/shard_map/sub | solution.py:120
  (144 shorter events, 42.4 us)
Async XLA Ops:
  1.4 33.5 %all-to-all-start = ((f32[8,3,2,8,128]{4,3,2,1,0:T(8,128)}), f32[8,3,2,8,128]{4,3,2,1,0:T(8,128)S(1)}, u32[]{:S(2)}, u32[]{:S(2)}) async-start(f32[8,3,2,8,128]{4,3,2,1,0:T(8,128)} %broadcast_in_dim.25), calls=%async_computation | async-start | bytes 393216 | tf_op jit(solution)/shard_map/all_to_all | solution.py:17
  7.4 9.2 %copy-start = (f32[12,16,8,128]{3,2,1,0:T(8,128)S(1)}, f32[12,16,8,128]{3,2,1,0:T(8,128)}, u32[]{:S(2)}) copy-start(f32[12,16,8,128]{3,2,1,0:T(8,128)} %param.8) | copy-start | bytes 2359300
  9.5 45.1 %collective-permute-start.2 = (f32[12,16,2,128]{3,1,2,0:T(8,128)}, f32[12,16,2,128]{3,1,2,0:T(8,128)}, u32[]{:S(2)}, u32[]{:S(2)}) collective-permute-start(f32[12,16,2,128]{3,1,2,0:T(8,128)} %get-tuple-element.20), channel_id=1, source_target_pairs={{0,8},{8,16},{16,24},{1,9},{9,17},{17,25},{2,10},{10,18},{18,26},{... | collective-permute-start | bytes 589832 | tf_op jit(solution)/shard_map/ppermute | solution.py:32
  11.4 50.9 %collective-permute-start.3 = (f32[12,16,2,128]{3,1,2,0:T(8,128)}, f32[12,16,2,128]{3,1,2,0:T(8,128)}, u32[]{:S(2)}, u32[]{:S(2)}) collective-permute-start(f32[12,16,2,128]{3,1,2,0:T(8,128)} %get-tuple-element.19), channel_id=1, source_target_pairs={{8,0},{16,8},{24,16},{9,1},{17,9},{25,17},{10,2},{18,10},{26,18},{... | collective-permute-start | bytes 589832 | tf_op jit(solution)/shard_map/ppermute | solution.py:33
  16.9 8.4 %copy-start.27 = (s32[8,128]{1,0:T(8,128)S(1)}, s32[8,128]{1,0:T(8,128)}, u32[]{:S(2)}) copy-start(s32[8,128]{1,0:T(8,128)} %param.12) | copy-start | bytes 12292
  17.5 8.9 %collective-permute-start.6 = (f32[12,16,8,2]{1,2,3,0:T(8,128)S(1)}, f32[12,16,8,2]{1,2,3,0:T(8,128)}, u32[]{:S(2)}, u32[]{:S(2)}) collective-permute-start(f32[12,16,8,2]{1,2,3,0:T(8,128)S(1)} %copy.141), channel_id=1, source_target_pairs={{0,1},{1,2},{2,3},{3,4},{4,5},{5,6},{6,7},{8,9},{9,10},{10,11},{11... | collective-permute-start | bytes 36872 | tf_op jit(solution)/shard_map/ppermute | solution.py:32
  21.1 10.0 %collective-permute-start.7 = (f32[12,16,8,2]{1,2,3,0:T(8,128)S(1)}, f32[12,16,8,2]{1,2,3,0:T(8,128)S(1)}, u32[]{:S(2)}, u32[]{:S(2)}) collective-permute-start(f32[12,16,8,2]{1,2,3,0:T(8,128)S(1)} %copy.142), channel_id=1, source_target_pairs={{1,0},{2,1},{3,2},{4,3},{5,4},{6,5},{7,6},{9,8},{10,9},{11,10},{12... | collective-permute-start | bytes 36872 | tf_op jit(solution)/shard_map/ppermute | solution.py:33
  25.3 20.2 %copy-start.5 = (f32[19,8,128]{2,0,1:T(8,128)}, f32[19,8,128]{2,0,1:T(8,128)S(1)}, u32[]{:S(2)}) copy-start(f32[19,8,128]{2,0,1:T(8,128)S(1)} %fusion.45) | copy-start | bytes 233476
  36.5 29.4 %collective-permute-start = (f32[50,2,128]{2,0,1:T(8,128)}, f32[50,2,128]{2,0,1:T(8,128)S(1)}, u32[]{:S(2)}, u32[]{:S(2)}) collective-permute-start(f32[50,2,128]{2,0,1:T(8,128)} %get-tuple-element.27), channel_id=1, source_target_pairs={{0,8},{8,16},{16,24},{1,9},{9,17},{17,25},{2,10},{10,18},{18,26},{... | collective-permute-start | bytes 153608 | tf_op jit(solution)/shard_map/ppermute | solution.py:32
  38.4 27.5 %collective-permute-start.1 = (f32[50,2,128]{2,0,1:T(8,128)}, f32[50,2,128]{2,0,1:T(8,128)}, u32[]{:S(2)}, u32[]{:S(2)}) collective-permute-start(f32[50,2,128]{2,0,1:T(8,128)} %get-tuple-element.28), channel_id=1, source_target_pairs={{8,0},{16,8},{24,16},{9,1},{17,9},{25,17},{10,2},{18,10},{26,18},{... | collective-permute-start | bytes 153608 | tf_op jit(solution)/shard_map/ppermute | solution.py:33
  43.6 9.1 %collective-permute-start.4 = (f32[50,8,2]{2,0,1:T(8,128)S(1)}, f32[50,8,2]{2,0,1:T(8,128)S(1)}, u32[]{:S(2)}, u32[]{:S(2)}) collective-permute-start(f32[50,8,2]{2,0,1:T(8,128)S(1)} %get-tuple-element.25), channel_id=1, source_target_pairs={{0,1},{1,2},{2,3},{3,4},{4,5},{5,6},{6,7},{8,9},{9,10},{10,11},{11... | collective-permute-start | bytes 9608 | tf_op jit(solution)/shard_map/ppermute | solution.py:32
  52.7 13.2 %collective-permute-start.5 = (f32[50,8,2]{2,0,1:T(8,128)}, f32[50,8,2]{2,0,1:T(8,128)}, u32[]{:S(2)}, u32[]{:S(2)}) collective-permute-start(f32[50,8,2]{2,0,1:T(8,128)} %get-tuple-element.26), channel_id=1, source_target_pairs={{1,0},{2,1},{3,2},{4,3},{5,4},{6,5},{7,6},{9,8},{10,9},{11,10},{12... | collective-permute-start | bytes 9608 | tf_op jit(solution)/shard_map/ppermute | solution.py:33
  56.6 18.7 %all-to-all-start.1 = ((f32[8,16,8,128]{3,2,1,0:T(8,128)}), f32[8,16,8,128]{3,2,1,0:T(8,128)}, u32[]{:S(2)}, u32[]{:S(2)}) async-start(f32[8,16,8,128]{3,2,1,0:T(8,128)} %broadcast_in_dim.31), calls=%async_computation.1 | async-start | bytes 1048576 | tf_op jit(solution)/shard_map/all_to_all | solution.py:17
  70.0 2.6 %copy-start.13 = (f32[16,9,128]{2,0,1:T(8,128)}, f32[16,9,128]{2,0,1:T(8,128)S(1)}, u32[]{:S(2)}) copy-start(f32[16,9,128]{2,0,1:T(8,128)S(1)} %get-tuple-element.8) | copy-start | bytes 221188
  70.0 2.6 %copy-start.23 = (pred[16,9,128]{2,0,1:T(8,128)(4,1)}, pred[16,9,128]{2,0,1:T(8,128)(4,1)S(1)}, u32[]{:S(2)}) copy-start(pred[16,9,128]{2,0,1:T(8,128)(4,1)S(1)} %get-tuple-element.7) | copy-start | bytes 55300
  72.7 3.9 %copy-start.19 = (f32[16,8,128]{2,1,0:T(8,128)S(1)}, f32[16,8,128]{2,1,0:T(8,128)}, u32[]{:S(2)}) copy-start(f32[16,8,128]{2,1,0:T(8,128)} %param.13) | copy-start | bytes 196612
  82.0 34.9 %collective-permute-start.8 = (f32[12,16,2,128]{3,1,2,0:T(8,128)}, f32[12,16,2,128]{3,1,2,0:T(8,128)S(1)}, u32[]{:S(2)}, u32[]{:S(2)}) collective-permute-start(f32[12,16,2,128]{3,1,2,0:T(8,128)} %get-tuple-element.15), channel_id=1, source_target_pairs={{0,8},{8,16},{16,24},{1,9},{9,17},{17,25},{2,10},{10,18},{18,26},{... | collective-permute-start | bytes 589832 | tf_op jit(solution)/shard_map/ppermute | solution.py:32
  83.9 33.0 %collective-permute-start.9 = (f32[12,16,2,128]{3,1,2,0:T(8,128)}, f32[12,16,2,128]{3,1,2,0:T(8,128)S(1)}, u32[]{:S(2)}, u32[]{:S(2)}) collective-permute-start(f32[12,16,2,128]{3,1,2,0:T(8,128)} %get-tuple-element.16), channel_id=1, source_target_pairs={{8,0},{16,8},{24,16},{9,1},{17,9},{25,17},{10,2},{18,10},{26,18},{... | collective-permute-start | bytes 589832 | tf_op jit(solution)/shard_map/ppermute | solution.py:33
  91.4 18.1 %collective-permute-start.10 = (f32[12,16,8,2]{1,2,3,0:T(8,128)}, f32[12,16,8,2]{1,2,3,0:T(8,128)}, u32[]{:S(2)}, u32[]{:S(2)}) collective-permute-start(f32[12,16,8,2]{1,2,3,0:T(8,128)} %copy.132), channel_id=1, source_target_pairs={{0,1},{1,2},{2,3},{3,4},{4,5},{5,6},{6,7},{8,9},{9,10},{10,11},{11... | collective-permute-start | bytes 36872 | tf_op jit(solution)/shard_map/ppermute | solution.py:32
  97.8 3.7 %copy-start.12 = (f32[17,8,128]{2,0,1:T(8,128)S(1)}, f32[17,8,128]{2,0,1:T(8,128)}, u32[]{:S(2)}) copy-start(f32[17,8,128]{2,0,1:T(8,128)} %copy-done.11) | copy-start | bytes 208900
  97.8 3.7 %copy-start.22 = (pred[17,8,128]{2,0,1:T(8,128)(4,1)S(1)}, pred[17,8,128]{2,0,1:T(8,128)(4,1)}, u32[]{:S(2)}) copy-start(pred[17,8,128]{2,0,1:T(8,128)(4,1)} %copy-done.21) | copy-start | bytes 52228
  97.8 15.4 %collective-permute-start.11 = (f32[12,16,8,2]{1,2,3,0:T(8,128)}, f32[12,16,8,2]{1,2,3,0:T(8,128)}, u32[]{:S(2)}, u32[]{:S(2)}) collective-permute-start(f32[12,16,8,2]{1,2,3,0:T(8,128)} %copy.134), channel_id=1, source_target_pairs={{1,0},{2,1},{3,2},{4,3},{5,4},{6,5},{7,6},{9,8},{10,9},{11,10},{12... | collective-permute-start | bytes 36872 | tf_op jit(solution)/shard_map/ppermute | solution.py:33
  103.8 19.7 %all-to-all-start.2 = ((f32[8,16,8,128]{3,2,1,0:T(8,128)}), f32[8,16,8,128]{3,2,1,0:T(8,128)S(1)}, u32[]{:S(2)}, u32[]{:S(2)}) async-start(f32[8,16,8,128]{3,2,1,0:T(8,128)} %broadcast_in_dim.32), calls=%async_computation.2 | async-start | bytes 1048576 | tf_op jit(solution)/shard_map/all_to_all | solution.py:17
  120.8 2.7 %copy-start.20 = (f32[16,8,128]{2,1,0:T(8,128)S(1)}, f32[16,8,128]{2,1,0:T(8,128)}, u32[]{:S(2)}) copy-start(f32[16,8,128]{2,1,0:T(8,128)} %param.13) | copy-start | bytes 196612
  (21 other events, 32.0 us)
where the time goes:
time: 130 us; the launch traced here: 129 us
  starting transfers between devices  56.7 us (44%)
  local copies, waits for them, and re-layouts  36.8 us (28%)
  other arithmetic  28.6 us (22%)
  waiting for transfers between devices  5.69 us (4%)
    ppermute x6, starting transfers between devices, with_halo(): lax.ppermute(initial, axis, [(b, a) for a, b in up])  24.9 us
    all_to_all x3, starting transfers between devices, from_everyone(): return lax.all_to_all(copies, axis, split_axis=0, concat_axis=0, tiled=True)  17.3 us
    ppermute x6, starting transfers between devices, with_halo(): lax.ppermute(last, axis, up)  14.5 us
    unnamed x67, local copies, waits for them, and re-layouts  9.89 us
    sub x4, other arithmetic, face_terms(): carried = carried - face_kappa * window(jump_face, 1, length + 2, direction)  8.86 us
    slice x6, local copies, waits for them, and re-layouts, with_halo(): last = lax.slice_in_dim(shard, length - width, length, axis=dim)  6.25 us
    ppermute x6, waiting for transfers between devices, with_halo(): lax.ppermute(last, axis, up)  5.67 us
    concatenate x4, other arithmetic, with_halo(): jnp.concatenate([jnp.pad(low, around), shard, jnp.pad(high, around)], axi...  4.92 us
  transfers between devices with their start and end apart: 15, of which 1 were waited for; matrix products, arithmetic and copies ran while one was open for 40% of the time, Pallas kernels for 0%

commit v1 on v0

v1 whole, which is shorter than its diff:
```python
import functools

import jax
import jax.numpy as jnp
from jax import lax
from jax.experimental import pallas as pl
from jax.experimental.pallas import tpu as pltpu
from jax.sharding import PartitionSpec as P

STEPS = 2
MESH = pl.DeviceIdType.MESH
F32 = jnp.float32
LANES = 128
LO, IN, HI = 6, 8, 16


def minmod(a, b):
    return jnp.maximum(0.0, jnp.minimum(a, b)) + jnp.minimum(0.0, jnp.maximum(a, b))


def roll(v, shift):
    return pltpu.roll(v, shift % LANES, 1)


def kernel(
    dims, tr, fl, de, dn, dep, gz, grp, prf, out,
    ext, adv, outv, flv, dev, dnv, depv, gzv, grps, prfs, tv,
    cxs, cxl, cxh, cys, cyl, cyh, fa, fb, fx,
    pqs, pqr, rs, rr, f1, f2, own1,
    sxl, sxh, xl, xh, yp, yl, yr, g1, g2,
    hy, fy, ky, hz, fz, hx, kx, wx, ec,
    lsem, csem, crec, fas, far, fbs, fbr, pqss, pqrs, rss, rrs, f1s, f1r, f2s, f2r,
    xss, xrs, yss, yrs, osem,
):
    nt, nx, ny, t_dev, lev, total = dims
    own = lev // nt
    me, gx, gy = lax.axis_index("tracer"), lax.axis_index("gx"), lax.axis_index("gy")
    left, right = lax.rem(gy + ny - 1, ny), lax.rem(gy + 1, ny)
    has_lo, has_hi = gx > 0, gx < nx - 1
    others = [lax.rem(me + d, nt) for d in range(1, nt)]

    loads = [
        (tr, ext.at[0, :, :, pl.ds(IN, 8), :]), (fl, flv), (de, dev), (dn, dnv), (dep, depv),
        (gz, gzv), (grp, grps), (prf, prfs),
    ]
    loads = [pltpu.make_async_copy(a, b, lsem.at[i]) for i, (a, b) in enumerate(loads)]

    barrier = pltpu.get_barrier_semaphore()
    for peer in others:
        pl.semaphore_signal(barrier, inc=1, device_id={"tracer": peer}, device_id_type=MESH)
    for z in (left, right):
        pl.semaphore_signal(barrier, inc=1, device_id={"gy": z}, device_id_type=MESH)

    @pl.when(has_lo)
    def _():
        pl.semaphore_signal(barrier, inc=1, device_id={"gx": gx - 1}, device_id_type=MESH)

    @pl.when(has_hi)
    def _():
        pl.semaphore_signal(barrier, inc=1, device_id={"gx": gx + 1}, device_id_type=MESH)

    for c in loads:
        c.start()

    lane = lax.broadcasted_iota(jnp.int32, (8, LANES), 1)
    row = lax.broadcasted_iota(jnp.int32, (8, LANES), 0)
    quad, e = lane // 4, lane % 4
    plev = quad % lev
    lane0, lane127 = lane == 0, lane == LANES - 1
    zero = jnp.zeros((8, LANES), F32)

    def spread(v):
        base = jnp.where(lane < 4, roll(v, 2), zero)
        for s in (4, 8, 16, 32, 64):
            base = base + roll(base, s)
        return base

    for c in loads[1:]:
        c.wait()
    for t in range(t_dev):
        tv[t] = jnp.full((8, LANES), prfs[grps[t]], F32)
    depth = depv[...].astype(F32)
    cxs[0] = depth
    cxs[1] = dev[...]
    rows_tile = zero
    lanes_tile = zero
    for b in range(own):
        rows_tile = jnp.where(row == b, flv[0, b, pl.ds(7, 1), :], rows_tile)
        col = spread(flv[1, b])
        lanes_tile = jnp.where((plev == me * own + b) & (e == 2), roll(col, 1), lanes_tile)
    cxs[2] = rows_tile
    cys[0] = spread(depth)
    cys[1] = spread(dnv[...])
    cys[2] = lanes_tile
    for k in range(3):
        for b in range(own):
            fa[me, k * own + b] = flv[k, b]
    fa[me, 3 * own] = lanes_tile
    loads[0].wait()

    def send(src, dst, ssem, rsem, to):
        return pltpu.make_async_remote_copy(
            src_ref=src, dst_ref=dst, send_sem=ssem, recv_sem=rsem, device_id=to, device_id_type=MESH
        )

    def pack_level(s, l, tiles, acc):
        acc = list(acc)
        for t in range(t_dev):
            sxl[s, l, pl.ds(2 * t, 2), :] = ext[s, t, l, pl.ds(IN, 2), :]
            sxh[s, l, pl.ds(2 * t, 2), :] = ext[s, t, l, pl.ds(IN + 6, 2), :]
            q = (t % 2) * lev + l
            acc[t // 2] = jnp.where(quad == q, pltpu.roll(tiles[t], lax.rem(4 * q + 2, LANES), 1), acc[t // 2])
        return tuple(acc)

    def first(l, acc):
        tiles = [ext[0, t, l, pl.ds(IN, 8), :] for t in range(t_dev)]
        p_sum, q_sum = zero, zero
        for t in range(t_dev):
            w = tv[t]
            wc = w * tiles[t]
            p_sum = p_sum + wc
            q_sum = q_sum + w * wc
        j, b = l // own, lax.rem(l, own)
        pqs[j, b] = p_sum
        pqs[j, own + b] = q_sum
        return pack_level(0, l, tiles, acc)

    acc = lax.fori_loop(0, lev, first, tuple(zero for _ in range(t_dev // 2)))
    for p in range(t_dev // 2):
        yp[0, p] = acc[p]

    pl.semaphore_wait(barrier, nt - 1 + 2 + has_lo.astype(jnp.int32) + has_hi.astype(jnp.int32))

    c_right = send(cys, cyl, csem.at[0], crec.at[0], {"gy": right})
    c_left = send(cys.at[pl.ds(0, 1)], cyh, csem.at[1], crec.at[1], {"gy": left})
    c_up = send(cxs, cxl, csem.at[2], crec.at[2], {"gx": gx + 1})
    c_down = send(cxs.at[pl.ds(0, 1)], cxh, csem.at[3], crec.at[3], {"gx": gx - 1})
    c_right.start()
    c_left.start()
    pl.when(has_hi)(c_up.start)
    pl.when(has_lo)(c_down.start)

    def y_copies(s):
        return (
            send(yp.at[s], yl.at[s], yss.at[s, 0], yrs.at[s, 0], {"gy": right}),
            send(yp.at[s], yr.at[s], yss.at[s, 1], yrs.at[s, 1], {"gy": left}),
        )

    def x_copies(s, j):
        c = pl.ds(j * own, own)
        return (
            send(sxh.at[s, c], xl.at[s, c], xss.at[s, 0, j], xrs.at[s, 0, j], {"gx": gx + 1}),
            send(sxl.at[s, c], xh.at[s, c], xss.at[s, 1, j], xrs.at[s, 1, j], {"gx": gx - 1}),
        )

    def gather_start(buf, ssem, rsem):
        for d, peer in enumerate(others):
            send(buf.at[me], buf.at[me], ssem.at[d], rsem.at[me], {"tracer": peer}).start()

    def gather_wait(buf, ssem, rsem):
        for d, peer in enumerate(others):
            send(buf.at[me], buf.at[peer], ssem.at[d], rsem.at[peer], {"tracer": peer}).wait_recv()

    def gather_done(buf, ssem, rsem):
        for d, peer in enumerate(others):
            send(buf.at[me], buf.at[peer], ssem.at[d], rsem.at[peer], {"tracer": peer}).wait_send()

    def scatter(src, dst, ssem, rsem, peer):
        return send(src.at[peer], dst.at[me], ssem.at[peer], rsem.at[me], {"tracer": peer})

    def scatter_wait(src, dst, ssem, rsem):
        for peer in others:
            send(src.at[peer], dst.at[peer], ssem.at[peer], rsem.at[peer], {"tracer": peer}).wait_recv()

    for peer in others:
        scatter(pqs, pqr, pqss, pqrs, peer).start()
    gather_start(fa, fas, far)
    for c in y_copies(0):
        c.start()

    def x_start(s, j):
        up, down = x_copies(s, j)
        pl.when(has_hi)(up.start)
        pl.when(has_lo)(down.start)

    for j in range(nt):
        x_start(0, j)

    c_right.wait_recv()
    c_left.wait_recv()
    pl.when(has_hi)(c_down.wait_recv)

    @pl.when(has_lo)
    def _():
        c_up.wait_recv()

    @pl.when(gx == 0)
    def _():
        for k in range(3):
            cxl[k] = zero

    @pl.when(gx == nx - 1)
    def _():
        cxh[0] = zero

    fb[me, 0] = cxl[2]
    fb[me, 1] = cyl[2]
    gather_start(fb, fbs, fbr)

    for k in range(2 * own):
        pqr[me, k] = pqs[me, k]
    scatter_wait(pqs, pqr, pqss, pqrs)
    scale = 4.0 / total
    for b in range(own):
        prey = pqr[0, b]
        sq = pqr[0, own + b]
        for j in range(1, nt):
            prey = prey + pqr[j, b]
            sq = sq + pqr[j, own + b]
        f1[me, b] = gzv[me * own + b] / (1.0 + scale * prey)
        own1[b] = sq
    gather_start(f1, f1s, f1r)

    dep_l = cyl[0] * (gy > 0).astype(F32)
    dep_r = cyh[0] * (gy < ny - 1).astype(F32)
    dep_m = cys[0]
    plevf = plev.astype(F32)
    wet0 = (plevf < jnp.where(e < 2, dep_l, dep_m)).astype(F32)
    wet1 = (plevf < jnp.where(e < 2, dep_m, dep_r)).astype(F32)
    open0 = wet0 * roll(wet0, 1)
    open1 = wet1 * roll(wet1, 1)
    wx[...] = jnp.zeros_like(wx)
    wx[pl.ds(LO, 2), :] = cxl[0, pl.ds(6, 2), :]
    wx[pl.ds(IN, 8), :] = depth
    wx[pl.ds(HI, 2), :] = cxh[0, pl.ds(0, 2), :]
    gather_wait(fa, fas, far)
    flux_edge = fa[0, 3 * own]
    for j in range(1, nt):
        flux_edge = flux_edge + fa[j, 3 * own]
    ec[0] = 0.5 * open0
    ec[2] = 2.0 * open0 * roll(cyl[1], 1)
    ec[3] = 0.5 * open1
    ec[4] = flux_edge * open1
    ec[5] = 2.0 * open1 * roll(cys[1], 1)
    dn_low = 2.0 * roll(dnv[...], 1)
    depth_y = jnp.minimum(depth, roll(depth, 1))

    for l in range(lev):
        j, b = l // own, l % own
        open_y = (depth_y > l).astype(F32)
        hy[l] = 0.5 * open_y
        fy[l] = roll(fa[j, own + b], 1) * open_y
        ky[l] = dn_low * open_y
        if l:
            open_z = (depth > l).astype(F32)
            hz[l] = 0.5 * open_z
            fz[l] = fa[(l - 1) // own, 2 * own + (l - 1) % own] * open_z
        fx[l, pl.ds(IN, 8), :] = fa[j, b]

    def edge(cells, h, flux, kappa):
        below = roll(cells, 1)
        jump = h * (cells - below)
        slope = minmod(jump, roll(jump, -1))
        carried = flux * jnp.where(flux > 0.0, below + roll(slope, 1), cells - slope) - kappa * jump
        return jump, carried

    def y_edges(s):
        for c in y_copies(s):
            c.wait_recv()
        for p in range(t_dev // 2):
            mine = yp[s, p]
            j0, c0 = edge(jnp.where(e < 2, yl[s, p], mine), ec[0], ec[1], ec[2])
            j1, c1 = edge(jnp.where(e < 2, mine, yr[s, p]), ec[3], ec[4], ec[5])
            g1[p] = jnp.where(e == 0, roll(j1, -2), roll(j0, -1))
            g2[p] = jnp.where(e == 0, roll(c1, -2), roll(c0, -1))

    def yz_part(s):
        def pair(p, carry):
            for h in range(2):
                t = 2 * p + h
                cells = [ext[s, t, l, pl.ds(IN, 8), :] for l in range(lev)]
                jumps = [zero] + [hz[l] * (cells[l] - cells[l - 1]) for l in range(1, lev)] + [zero]
                slopes = [minmod(jumps[l], jumps[l + 1]) for l in range(lev)]
                faces = [zero]
                for l in range(1, lev):
                    f = fz[l]
                    faces.append(f * jnp.where(f > 0.0, cells[l - 1] + slopes[l - 1], cells[l] - slopes[l]))
                faces.append(zero)
                for l in range(lev):
                    q = h * lev + l
                    c = cells[l]
                    e1 = roll(g1[p], -(4 * q + 1))
                    e2 = roll(g2[p], -(4 * q + 1))
                    below = roll(c, 1)
                    f = fy[l]
                    jump = jnp.where(lane0, e1, hy[l] * (c - below))
                    jump_up = jnp.where(lane127, e1, roll(jump, -1))
                    slope = minmod(jump, jump_up)
                    carried = f * jnp.where(f > 0.0, below + roll(slope, 1), c - slope) - ky[l] * jump
                    carried = jnp.where(lane0, e2, carried)
                    carried_up = jnp.where(lane127, e2, roll(carried, -1))
                    adv[t, l] = c + ((carried - carried_up) + (faces[l] - faces[l + 1]))
            return carry

        lax.fori_loop(0, t_dev // 2, pair, 0)

    def x_part(s, reduce_r):
        def chunk(j, carry):
            up, down = x_copies(s, j)
            pl.when(has_lo)(up.wait_recv)
            pl.when(has_hi)(down.wait_recv)
            for b in range(own):
                l = j * own + b
                h = [hx[l, pl.ds(IN - 1 + k, 8), :] for k in range(4)]
                f = [fx[l, pl.ds(IN - 1 + k, 8), :] for k in range(2)]
                kk = [kx[l, pl.ds(IN + k, 8), :] for k in range(2)]
                total_r = zero
                for t in range(t_dev):
                    ext[s, t, l, pl.ds(LO, 2), :] = xl[s, l, pl.ds(2 * t, 2), :]
                    ext[s, t, l, pl.ds(HI, 2), :] = xh[s, l, pl.ds(2 * t, 2), :]
                    c = [ext[s, t, l, pl.ds(LO + k, 8), :] for k in range(5)]
                    jump = [h[k] * (c[k + 1] - c[k]) for k in range(4)]
                    slope = [minmod(jump[k], jump[k + 1]) for k in range(3)]
                    carried = [
                        f[k] * jnp.where(f[k] > 0.0, c[k + 1] + slope[k], c[k + 2] - slope[k + 1])
                        - kk[k] * jump[k + 1]
                        for k in range(2)
                    ]
                    a = adv[t, l] + (carried[0] - carried[1])
                    adv[t, l] = a
                    if reduce_r:
                        total_r = total_r + tv[t] * a
                if reduce_r:
                    rs[j, b] = total_r
            if reduce_r:
                @pl.when(j != me)
                def _():
                    scatter(rs, rr, rss, rrs, j).start()
            return carry

        lax.fori_loop(0, nt, chunk, 0)

    for s in range(STEPS):
        @pl.when(gx == 0)
        def _():
            xl[s] = jnp.zeros_like(xl[s])

        @pl.when(gx == nx - 1)
        def _():
            xh[s] = jnp.zeros_like(xh[s])

    gather_wait(fb, fbs, fbr)
    flux_edge = fb[0, 1]
    for j in range(1, nt):
        flux_edge = flux_edge + fb[j, 1]
    ec[1] = flux_edge * open0
    for l in range(lev):
        fx[l, pl.ds(IN - 1, 1), :] = fb[l // own, 0, pl.ds(l % own, 1), :]
    d_low = jnp.concatenate([2.0 * cxl[1, pl.ds(7, 1), :], 2.0 * dev[pl.ds(0, 7), :]], axis=0)
    d_up = 2.0 * dev[...]
    depth_x = [
        jnp.minimum(wx[pl.ds(LO + k, 8), :], wx[pl.ds(LO + 1 + k, 8), :]) for k in range(4)
    ]
    for l in range(lev):
        opens = [(depth_x[k] > l).astype(F32) for k in range(4)]
        low = fx[l, pl.ds(IN - 1, 8), :] * opens[1]
        up = fx[l, pl.ds(IN, 8), :] * opens[2]
        hx[l, pl.ds(IN - 1, 8), :] = 0.5 * opens[0]
        hx[l, pl.ds(IN + 2, 8), :] = 0.5 * opens[3]
        fx[l, pl.ds(IN - 1, 8), :] = low
        fx[l, pl.ds(IN, 8), :] = up
        kx[l, pl.ds(IN, 8), :] = d_low * opens[1]
        kx[l, pl.ds(IN + 1, 8), :] = d_up * opens[2]

    y_edges(0)
    yz_part(0)
    x_part(0, True)
    gather_wait(f1, f1s, f1r)

    def second(l, acc):
        j, b = l // own, lax.rem(l, own)
        factor = f1[j, b]
        tiles = []
        for t in range(t_dev):
            c = adv[t, l] - (tv[t] * factor) * ext[0, t, l, pl.ds(IN, 8), :]
            ext[1, t, l, pl.ds(IN, 8), :] = c
            tiles.append(c)
        return pack_level(1, l, tiles, acc)

    acc = lax.fori_loop(0, lev, second, tuple(zero for _ in range(t_dev // 2)))
    for p in range(t_dev // 2):
        yp[1, p] = acc[p]
    for c in y_copies(1):
        c.start()
    for j in range(nt):
        x_start(1, j)

    for b in range(own):
        rr[me, b] = rs[me, b]
    scatter_wait(rs, rr, rss, rrs)
    for b in range(own):
        prey = rr[0, b]
        for j in range(1, nt):
            prey = prey + rr[j, b]
        prey = prey - f1[me, b] * own1[b]
        f2[me, b] = gzv[me * own + b] / (1.0 + scale * prey)
    gather_start(f2, f2s, f2r)

    y_edges(1)
    yz_part(1)
    x_part(1, False)
    gather_wait(f2, f2s, f2r)

    def last(l, carry):
        j, b = l // own, lax.rem(l, own)
        factor = f2[j, b]
        for t in range(t_dev):
            outv[t, l] = adv[t, l] - (tv[t] * factor) * ext[1, t, l, pl.ds(IN, 8), :]
        return carry

    lax.fori_loop(0, lev, last, 0)
    store = pltpu.make_async_copy(outv, out, osem)
    store.start()

    c_right.wait_send()
    c_left.wait_send()
    pl.when(has_hi)(c_up.wait_send)
    pl.when(has_lo)(c_down.wait_send)
    for s in range(STEPS):
        for c in y_copies(s):
            c.wait_send()
        for j in range(nt):
            up, down = x_copies(s, j)
            pl.when(has_hi)(up.wait_send)
            pl.when(has_lo)(down.wait_send)
    gather_done(fa, fas, far)
    gather_done(fb, fbs, fbr)
    gather_done(f1, f1s, f1r)
    gather_done(f2, f2s, f2r)
    for peer in others:
        scatter(pqs, pqr, pqss, pqrs, peer).wait_send()
        scatter(rs, rr, rss, rrs, peer).wait_send()
    store.wait()


def on_device(tracers, fluxes, diff_east, diff_north, column_depth, grazers, groups, preference):
    t_dev, lev, rows, cols = tracers.shape
    nt, nx, ny = (lax.axis_size(a) for a in ("tracer", "gx", "gy"))
    own = lev // nt
    tile = (8, LANES)
    half = t_dev // 2
    dma = pltpu.SemaphoreType.DMA

    def v(*shape):
        return pltpu.VMEM(shape, F32)

    scratch = [
        v(2, t_dev, lev, 24, LANES), v(t_dev, lev, *tile), v(t_dev, lev, *tile),
        v(3, own, *tile), v(*tile), v(*tile), pltpu.VMEM(tile, jnp.int32), v(lev, *tile),
        pltpu.SMEM(groups.shape, jnp.int32), pltpu.SMEM(preference.shape, F32), v(t_dev, *tile),
        v(3, *tile), v(3, *tile), v(1, *tile), v(3, *tile), v(3, *tile), v(1, *tile),
        v(nt, 3 * own + 1, *tile), v(nt, 2, *tile), v(lev, 24, LANES),
        v(nt, 2 * own, *tile), v(nt, 2 * own, *tile), v(nt, own, *tile), v(nt, own, *tile),
        v(nt, own, *tile), v(nt, own, *tile), v(own, *tile),
        v(2, lev, 2 * t_dev, LANES), v(2, lev, 2 * t_dev, LANES),
        v(2, lev, 2 * t_dev, LANES), v(2, lev, 2 * t_dev, LANES),
        v(2, half, *tile), v(2, half, *tile), v(2, half, *tile), v(half, *tile), v(half, *tile),
        v(lev, *tile), v(lev, *tile), v(lev, *tile), v(lev, *tile), v(lev, *tile),
        v(lev, 24, LANES), v(lev, 24, LANES), v(24, LANES), v(6, *tile),
        dma((8,)), dma((4,)), dma((4,)),
        dma((nt,)), dma((nt,)), dma((nt,)), dma((nt,)), dma((nt,)), dma((nt,)),
        dma((nt,)), dma((nt,)), dma((nt,)), dma((nt,)), dma((nt,)), dma((nt,)),
        dma((2, 2, nt)), dma((2, 2, nt)), dma((2, 2)), dma((2, 2)), dma,
    ]
    return pl.pallas_call(
        functools.partial(kernel, (nt, nx, ny, t_dev, lev, t_dev * nt)),
        out_shape=jax.ShapeDtypeStruct(tracers.shape, F32),
        in_specs=[pl.BlockSpec(memory_space=pl.ANY)] * 8,
        out_specs=pl.BlockSpec(memory_space=pl.ANY),
        scratch_shapes=scratch,
        compiler_params=pltpu.CompilerParams(collective_id=0, has_side_effects=True),
        name="plankton",
    )(tracers, fluxes, diff_east, diff_north, column_depth, grazers, groups, preference)


def solution(mesh):
    placed = (
        P("tracer", None, "gx", "gy"),
        P(None, "tracer", "gx", "gy"),
        P("gx", "gy"),
        P("gx", "gy"),
        P("gx", "gy"),
        P(None, "gx", "gy"),
        P("tracer"),
        P(),
    )
    return jax.shard_map(
        on_device,
        mesh=mesh,
        in_specs=placed,
        out_specs=P("tracer", None, "gx", "gy"),
        check_vma=False,
    )
```

time: 130 us -> 37.2 us (0.29)
  the two profiles are of different devices: /device:TPU:134 before, /device:TPU:1 now
where the time goes in v1:
time: 37.2 us; the launch traced here: 37.1 us
  Pallas kernels  35 us (94%)
  local copies, waits for them, and re-layouts  2.06 us (6%)
    pallas_call x1, Pallas kernels, on_device(): pl.pallas_call(functools.partial(kernel, (nt, nx, ny, t_dev, lev, t_dev *...  35 us
    unnamed x1, local copies, waits for them, and re-layouts  2.06 us

profile of v1, /device:TPU:1, one launch (start us, length us, event | category | flops | bytes accessed | tf_op | source)
XLA Modules:
  0.0 37.1 jit_solution(2487485805680712735)
XLA Ops:
  0.0 35.0 %plankton.1 = f32[12,16,8,128]{3,2,1,0:T(8,128)} custom-call(f32[12,16,8,128]{3,2,1,0:T(8,128)} %tr.1, f32[3,2,8,128]{3,2,1,0:T(8,128)} %fl.1, f32[8,128]{1,0:T(8,128)} %de.1, f32[8,128]{1,0:T(8,128)} %dn.1, s32[8,128]{1,0:T(8,128)} %dep.1, f32[16,8,128]{2,1,0:T(8,128)} %gz.1, s32[12]{0:T(128)} %grp.1, f32[16]{0:T(128)} %prf.1), custom_call_target="tpu_custom_call" | custom-call | tf_op jit(solution)/shard_map/plankton/pallas_call | solution.py:475
  35.0 2.1 %copy.10 = f32[12,16,8,128]{3,2,1,0:T(8,128)} copy(f32[12,16,8,128]{3,2,1,0:T(8,128)} %plankton.1) | data formatting | bytes 1572864

commit v2 on v1

--- a/solution.py
+++ b/solution.py
@@ -23,14 +23,14 @@
 
 
 def kernel(
-    dims, tr, fl, de, dn, dep, gz, grp, prf, out,
-    ext, adv, outv, flv, dev, dnv, depv, gzv, grps, prfs, tv,
+    dims, tr, fl, de, dn, dep, gz, grp, prf, adv, grazed, f2,
+    ext, flv, dev, dnv, depv, gzv, grps, prfs, tv,
     cxs, cxl, cxh, cys, cyl, cyh, fa, fb, fx,
-    pqs, pqr, rs, rr, f1, f2, own1,
-    sxl, sxh, xl, xh, yp, yl, yr, g1, g2,
+    pqs, pqr, rs, rr, f1, own1,
+    sxl, sxh, xl, xh, yp, yl, yr, ge, yst, gsl, gsh, gxl, gxh, tx,
     hy, fy, ky, hz, fz, hx, kx, wx, ec,
     lsem, csem, crec, fas, far, fbs, fbr, pqss, pqrs, rss, rrs, f1s, f1r, f2s, f2r,
-    xss, xrs, yss, yrs, osem,
+    xss, xrs, yss, yrs, gss, grs,
 ):
     nt, nx, ny, t_dev, lev, total = dims
     own = lev // nt
@@ -64,21 +64,22 @@
 
     lane = lax.broadcasted_iota(jnp.int32, (8, LANES), 1)
     row = lax.broadcasted_iota(jnp.int32, (8, LANES), 0)
-    quad, e = lane // 4, lane % 4
-    plev = quad % lev
-    lane0, lane127 = lane == 0, lane == LANES - 1
+    plev, e = lane // 8, lane % 8
+    at_edge = (lane < 2) | (lane >= LANES - 2)
     zero = jnp.zeros((8, LANES), F32)
 
     def spread(v):
-        base = jnp.where(lane < 4, roll(v, 2), zero)
-        for s in (4, 8, 16, 32, 64):
+        base = jnp.where(lane < 8, roll(v, 4), zero)
+        for s in (8, 16, 32, 64):
             base = base + roll(base, s)
         return base
 
     for c in loads[1:]:
         c.wait()
     for t in range(t_dev):
-        tv[t] = jnp.full((8, LANES), prfs[grps[t]], F32)
+        w = jnp.full((8, LANES), prfs[grps[t]], F32)
+        tv[t] = w
+        tx[t // 4] = w if t % 4 == 0 else jnp.where(row // 2 == t % 4, w, tx[t // 4])
     depth = depv[...].astype(F32)
     cxs[0] = depth
     cxs[1] = dev[...]
@@ -86,8 +87,7 @@
     lanes_tile = zero
     for b in range(own):
         rows_tile = jnp.where(row == b, flv[0, b, pl.ds(7, 1), :], rows_tile)
-        col = spread(flv[1, b])
-        lanes_tile = jnp.where((plev == me * own + b) & (e == 2), roll(col, 1), lanes_tile)
+        lanes_tile = jnp.where(plev == me * own + b, spread(flv[1, b]), lanes_tile)
     cxs[2] = rows_tile
     cys[0] = spread(depth)
     cys[1] = spread(dnv[...])
@@ -106,10 +106,10 @@
     def pack_level(s, l, tiles, acc):
         acc = list(acc)
         for t in range(t_dev):
-            sxl[s, l, pl.ds(2 * t, 2), :] = ext[s, t, l, pl.ds(IN, 2), :]
-            sxh[s, l, pl.ds(2 * t, 2), :] = ext[s, t, l, pl.ds(IN + 6, 2), :]
-            q = (t % 2) * lev + l
-            acc[t // 2] = jnp.where(quad == q, pltpu.roll(tiles[t], lax.rem(4 * q + 2, LANES), 1), acc[t // 2])
+            if s == 0:
+                sxl[s, l, pl.ds(2 * t, 2), :] = ext[s, t, l, pl.ds(IN, 2), :]
+                sxh[s, l, pl.ds(2 * t, 2), :] = ext[s, t, l, pl.ds(IN + 6, 2), :]
+            acc[t] = jnp.where(plev == l, pltpu.roll(tiles[t], 8 * l + 4, 1), acc[t])
         return tuple(acc)
 
     def first(l, acc):
@@ -125,9 +125,9 @@
         pqs[j, own + b] = q_sum
         return pack_level(0, l, tiles, acc)
 
-    acc = lax.fori_loop(0, lev, first, tuple(zero for _ in range(t_dev // 2)))
-    for p in range(t_dev // 2):
-        yp[0, p] = acc[p]
+    acc = lax.fori_loop(0, lev, first, tuple(zero for _ in range(t_dev)))
+    for t in range(t_dev):
+        yp[0, t] = acc[t]
 
     pl.semaphore_wait(barrier, nt - 1 + 2 + has_lo.astype(jnp.int32) + has_hi.astype(jnp.int32))
 
@@ -207,6 +207,18 @@
     fb[me, 1] = cyl[2]
     gather_start(fb, fbs, fbr)
 
+    dep_l = cyl[0] * (gy > 0).astype(F32)
+    dep_r = cyh[0] * (gy < ny - 1).astype(F32)
+    dep_m = cys[0]
+    plevf = plev.astype(F32)
+    wet0 = (plevf < jnp.where(e < 4, dep_l, dep_m)).astype(F32)
+    wet1 = (plevf < jnp.where(e < 4, dep_m, dep_r)).astype(F32)
+    open0 = wet0 * roll(wet0, 1)
+    open1 = wet1 * roll(wet1, 1)
+    wx[...] = jnp.zeros_like(wx)
+    wx[pl.ds(LO, 2), :] = cxl[0, pl.ds(6, 2), :]
+    wx[pl.ds(IN, 8), :] = depth
+    wx[pl.ds(HI, 2), :] = cxh[0, pl.ds(0, 2), :]
     for k in range(2 * own):
         pqr[me, k] = pqs[me, k]
     scatter_wait(pqs, pqr, pqss, pqrs)
@@ -221,26 +233,15 @@
         own1[b] = sq
     gather_start(f1, f1s, f1r)
 
-    dep_l = cyl[0] * (gy > 0).astype(F32)
-    dep_r = cyh[0] * (gy < ny - 1).astype(F32)
-    dep_m = cys[0]
-    plevf = plev.astype(F32)
-    wet0 = (plevf < jnp.where(e < 2, dep_l, dep_m)).astype(F32)
-    wet1 = (plevf < jnp.where(e < 2, dep_m, dep_r)).astype(F32)
-    open0 = wet0 * roll(wet0, 1)
-    open1 = wet1 * roll(wet1, 1)
-    wx[...] = jnp.zeros_like(wx)
-    wx[pl.ds(LO, 2), :] = cxl[0, pl.ds(6, 2), :]
-    wx[pl.ds(IN, 8), :] = depth
-    wx[pl.ds(HI, 2), :] = cxh[0, pl.ds(0, 2), :]
     gather_wait(fa, fas, far)
     flux_edge = fa[0, 3 * own]
     for j in range(1, nt):
         flux_edge = flux_edge + fa[j, 3 * own]
     ec[0] = 0.5 * open0
-    ec[2] = 2.0 * open0 * roll(cyl[1], 1)
+    ec[1] = flux_edge
+    ec[2] = 2.0 * open0 * roll(jnp.where(e < 4, cyl[1], cys[1]), 1)
     ec[3] = 0.5 * open1
-    ec[4] = flux_edge * open1
+    ec[4] = roll(flux_edge, 1) * open1
     ec[5] = 2.0 * open1 * roll(cys[1], 1)
     dn_low = 2.0 * roll(dnv[...], 1)
     depth_y = jnp.minimum(depth, roll(depth, 1))
@@ -262,19 +263,18 @@
         jump = h * (cells - below)
         slope = minmod(jump, roll(jump, -1))
         carried = flux * jnp.where(flux > 0.0, below + roll(slope, 1), cells - slope) - kappa * jump
-        return jump, carried
+        return carried - roll(carried, -1)
 
     def y_edges(s):
         for c in y_copies(s):
             c.wait_recv()
-        for p in range(t_dev // 2):
-            mine = yp[s, p]
-            j0, c0 = edge(jnp.where(e < 2, yl[s, p], mine), ec[0], ec[1], ec[2])
-            j1, c1 = edge(jnp.where(e < 2, mine, yr[s, p]), ec[3], ec[4], ec[5])
-            g1[p] = jnp.where(e == 0, roll(j1, -2), roll(j0, -1))
-            g2[p] = jnp.where(e == 0, roll(c1, -2), roll(c0, -1))
-
-    def yz_part(s):
+        for t in range(t_dev):
+            mine = yp[s, t]
+            low = edge(jnp.where(e < 4, yl[s, t], mine), ec[0], ec[1], ec[2])
+            high = edge(jnp.where(e < 4, mine, yr[s, t]), ec[3], ec[4], ec[5])
+            ge[t] = jnp.where(e < 4, high, low)
+
+    def z_part(s):
         def pair(p, carry):
             for h in range(2):
                 t = 2 * p + h
@@ -287,55 +287,90 @@
                     faces.append(f * jnp.where(f > 0.0, cells[l - 1] + slopes[l - 1], cells[l] - slopes[l]))
                 faces.append(zero)
                 for l in range(lev):
-                    q = h * lev + l
-                    c = cells[l]
-                    e1 = roll(g1[p], -(4 * q + 1))
-                    e2 = roll(g2[p], -(4 * q + 1))
-                    below = roll(c, 1)
-                    f = fy[l]
-                    jump = jnp.where(lane0, e1, hy[l] * (c - below))
-                    jump_up = jnp.where(lane127, e1, roll(jump, -1))
-                    slope = minmod(jump, jump_up)
-                    carried = f * jnp.where(f > 0.0, below + roll(slope, 1), c - slope) - ky[l] * jump
-                    carried = jnp.where(lane0, e2, carried)
-                    carried_up = jnp.where(lane127, e2, roll(carried, -1))
-                    adv[t, l] = c + ((carried - carried_up) + (faces[l] - faces[l + 1]))
+                    adv[t, l] = cells[l] + (faces[l] - faces[l + 1])
             return carry
 
         lax.fori_loop(0, t_dev // 2, pair, 0)
 
-    def x_part(s, reduce_r):
+    def y_part(s):
+        def slopes(l, slot):
+            h = hy[l]
+            h_up = roll(h, -1)
+            for t in range(t_dev):
+                c = ext[s, t, l, pl.ds(IN, 8), :]
+                jump = h * (c - roll(c, 1))
+                jump_up = h_up * (roll(c, -1) - c)
+                slope = minmod(jump, jump_up)
+                yst[slot, 0, t] = c + slope
+                yst[slot, 1, t] = c - slope
+                yst[slot, 2, t] = jump
+                yst[slot, 3, t] = jump_up
+
+        def fluxes(l, slot):
+            f, k = fy[l], ky[l]
+            f_up, k_up = roll(f, -1), roll(k, -1)
+            ahead, ahead_up = f > 0.0, f_up > 0.0
+            for t in range(t_dev):
+                fore, aft = yst[slot, 0, t], yst[slot, 1, t]
+                carried = f * jnp.where(ahead, roll(fore, 1), aft) - k * yst[slot, 2, t]
+                carried_up = f_up * jnp.where(ahead_up, fore, roll(aft, -1)) - k_up * yst[slot, 3, t]
+                outer = pltpu.roll(ge[t], (LANES - 4) - 8 * l, 1)
+                adv[t, l] = adv[t, l] + jnp.where(at_edge, outer, carried - carried_up)
+
+        def level(l, carry):
+            slopes(l, lax.rem(l, 2))
+            fluxes(l - 1, lax.rem(l + 1, 2))
+            return carry
+
+        slopes(0, 0)
+        lax.fori_loop(1, lev, level, 0)
+        fluxes(lev - 1, (lev - 1) % 2)
+
+    def x_part(s):
         def chunk(j, carry):
             up, down = x_copies(s, j)
             pl.when(has_lo)(up.wait_recv)
             pl.when(has_hi)(down.wait_recv)
             for b in range(own):
                 l = j * own + b
+                if s:
+                    for halo, fac in ((xl, gxl), (xh, gxh)):
+                        two = pl.multiple_of(2 * l, 2)
+                        f8 = jnp.where(row % 2 == 0, fac[pl.ds(two, 1), :], fac[pl.ds(two + 1, 1), :])
+                        for k in range(2 * t_dev // 8):
+                            r = pl.ds(8 * k, 8)
+                            halo[1, l, r, :] = halo[1, l, r, :] - (tx[k] * f8) * halo[0, l, r, :]
                 h = [hx[l, pl.ds(IN - 1 + k, 8), :] for k in range(4)]
                 f = [fx[l, pl.ds(IN - 1 + k, 8), :] for k in range(2)]
                 kk = [kx[l, pl.ds(IN + k, 8), :] for k in range(2)]
+                ahead = [f[k] > 0.0 for k in range(2)]
                 total_r = zero
                 for t in range(t_dev):
-                    ext[s, t, l, pl.ds(LO, 2), :] = xl[s, l, pl.ds(2 * t, 2), :]
-                    ext[s, t, l, pl.ds(HI, 2), :] = xh[s, l, pl.ds(2 * t, 2), :]
+                    two = pl.ds(2 * t, 2)
+                    ext[s, t, l, pl.ds(LO, 2), :] = xl[s, l, two, :]
+                    ext[s, t, l, pl.ds(HI, 2), :] = xh[s, l, two, :]
                     c = [ext[s, t, l, pl.ds(LO + k, 8), :] for k in range(5)]
                     jump = [h[k] * (c[k + 1] - c[k]) for k in range(4)]
                     slope = [minmod(jump[k], jump[k + 1]) for k in range(3)]
                     carried = [
-                        f[k] * jnp.where(f[k] > 0.0, c[k + 1] + slope[k], c[k + 2] - slope[k + 1])
+                        f[k] * jnp.where(ahead[k], c[k + 1] + slope[k], c[k + 2] - slope[k + 1])
                         - kk[k] * jump[k + 1]
                         for k in range(2)
                     ]
                     a = adv[t, l] + (carried[0] - carried[1])
                     adv[t, l] = a
-                    if reduce_r:
+                    if s == 0:
                         total_r = total_r + tv[t] * a
-                if reduce_r:
+                        sxl[1, l, two, :] = adv[t, l, pl.ds(0, 2), :]
+                        sxh[1, l, two, :] = adv[t, l, pl.ds(6, 2), :]
+                if s == 0:
                     rs[j, b] = total_r
-            if reduce_r:
+            if s == 0:
                 @pl.when(j != me)
                 def _():
                     scatter(rs, rr, rss, rrs, j).start()
+
+                x_start(1, j)
             return carry
 
         lax.fori_loop(0, nt, chunk, 0)
@@ -353,7 +388,7 @@
     flux_edge = fb[0, 1]
     for j in range(1, nt):
         flux_edge = flux_edge + fb[j, 1]
-    ec[1] = flux_edge * open0
+    ec[1] = roll(jnp.where(e < 4, flux_edge, ec[1]), 1) * open0
     for l in range(lev):
         fx[l, pl.ds(IN - 1, 1), :] = fb[l // own, 0, pl.ds(l % own, 1), :]
     d_low = jnp.concatenate([2.0 * cxl[1, pl.ds(7, 1), :], 2.0 * dev[pl.ds(0, 7), :]], axis=0)
@@ -372,10 +407,18 @@
         kx[l, pl.ds(IN, 8), :] = d_low * opens[1]
         kx[l, pl.ds(IN + 1, 8), :] = d_up * opens[2]
 
+    z_part(0)
     y_edges(0)
-    yz_part(0)
-    x_part(0, True)
+    y_part(0)
+    x_part(0)
     gather_wait(f1, f1s, f1r)
+    for l in range(lev):
+        gsl[pl.ds(2 * l, 2), :] = f1[l // own, l % own, pl.ds(0, 2), :]
+        gsh[pl.ds(2 * l, 2), :] = f1[l // own, l % own, pl.ds(6, 2), :]
+    g_up = send(gsh, gxl, gss.at[0], grs.at[0], {"gx": gx + 1})
+    g_down = send(gsl, gxh, gss.at[1], grs.at[1], {"gx": gx - 1})
+    pl.when(has_hi)(g_up.start)
+    pl.when(has_lo)(g_down.start)
 
     def second(l, acc):
         j, b = l // own, lax.rem(l, own)
@@ -384,16 +427,16 @@
         for t in range(t_dev):
             c = adv[t, l] - (tv[t] * factor) * ext[0, t, l, pl.ds(IN, 8), :]
             ext[1, t, l, pl.ds(IN, 8), :] = c
+            grazed[t, l] = tv[t] * c
             tiles.append(c)
         return pack_level(1, l, tiles, acc)
 
-    acc = lax.fori_loop(0, lev, second, tuple(zero for _ in range(t_dev // 2)))
-    for p in range(t_dev // 2):
-        yp[1, p] = acc[p]
+    acc = lax.fori_loop(0, lev, second, tuple(zero for _ in range(t_dev)))
+    for t in range(t_dev):
+        yp[1, t] = acc[t]
     for c in y_copies(1):
         c.start()
-    for j in range(nt):
-        x_start(1, j)
+    z_part(1)
 
     for b in range(own):
         rr[me, b] = rs[me, b]
@@ -407,25 +450,27 @@
     gather_start(f2, f2s, f2r)
 
     y_edges(1)
-    yz_part(1)
-    x_part(1, False)
+    y_part(1)
+    pl.when(has_lo)(g_up.wait_recv)
+    pl.when(has_hi)(g_down.wait_recv)
+
+    @pl.when(gx == 0)
+    def _():
+        gxl[...] = jnp.zeros_like(gxl)
+
+    @pl.when(gx == nx - 1)
+    def _():
+        gxh[...] = jnp.zeros_like(gxh)
+
+    x_part(1)
     gather_wait(f2, f2s, f2r)
-
-    def last(l, carry):
-        j, b = l // own, lax.rem(l, own)
-        factor = f2[j, b]
-        for t in range(t_dev):
-            outv[t, l] = adv[t, l] - (tv[t] * factor) * ext[1, t, l, pl.ds(IN, 8), :]
-        return carry
-
-    lax.fori_loop(0, lev, last, 0)
-    store = pltpu.make_async_copy(outv, out, osem)
-    store.start()
 
     c_right.wait_send()
     c_left.wait_send()
     pl.when(has_hi)(c_up.wait_send)
     pl.when(has_lo)(c_down.wait_send)
+    pl.when(has_hi)(g_up.wait_send)
+    pl.when(has_lo)(g_down.wait_send)
     for s in range(STEPS):
         for c in y_copies(s):
             c.wait_send()
@@ -440,7 +485,6 @@
     for peer in others:
         scatter(pqs, pqr, pqss, pqrs, peer).wait_send()
         scatter(rs, rr, rss, rrs, peer).wait_send()
-    store.wait()
 
 
 def on_device(tracers, fluxes, diff_east, diff_north, column_depth, grazers, groups, preference):
@@ -448,39 +492,49 @@
     nt, nx, ny = (lax.axis_size(a) for a in ("tracer", "gx", "gy"))
     own = lev // nt
     tile = (8, LANES)
-    half = t_dev // 2
     dma = pltpu.SemaphoreType.DMA
 
     def v(*shape):
         return pltpu.VMEM(shape, F32)
 
     scratch = [
-        v(2, t_dev, lev, 24, LANES), v(t_dev, lev, *tile), v(t_dev, lev, *tile),
+        v(2, t_dev, lev, 24, LANES),
         v(3, own, *tile), v(*tile), v(*tile), pltpu.VMEM(tile, jnp.int32), v(lev, *tile),
         pltpu.SMEM(groups.shape, jnp.int32), pltpu.SMEM(preference.shape, F32), v(t_dev, *tile),
         v(3, *tile), v(3, *tile), v(1, *tile), v(3, *tile), v(3, *tile), v(1, *tile),
         v(nt, 3 * own + 1, *tile), v(nt, 2, *tile), v(lev, 24, LANES),
         v(nt, 2 * own, *tile), v(nt, 2 * own, *tile), v(nt, own, *tile), v(nt, own, *tile),
-        v(nt, own, *tile), v(nt, own, *tile), v(own, *tile),
+        v(nt, own, *tile), v(own, *tile),
         v(2, lev, 2 * t_dev, LANES), v(2, lev, 2 * t_dev, LANES),
         v(2, lev, 2 * t_dev, LANES), v(2, lev, 2 * t_dev, LANES),
-        v(2, half, *tile), v(2, half, *tile), v(2, half, *tile), v(half, *tile), v(half, *tile),
+        v(2, t_dev, *tile), v(2, t_dev, *tile), v(2, t_dev, *tile), v(t_dev, *tile), v(2, 4, t_dev, *tile),
+        v(2 * lev, LANES), v(2 * lev, LANES), v(2 * lev, LANES), v(2 * lev, LANES), v(2 * t_dev // 8, *tile),
         v(lev, *tile), v(lev, *tile), v(lev, *tile), v(lev, *tile), v(lev, *tile),
         v(lev, 24, LANES), v(lev, 24, LANES), v(24, LANES), v(6, *tile),
         dma((8,)), dma((4,)), dma((4,)),
         dma((nt,)), dma((nt,)), dma((nt,)), dma((nt,)), dma((nt,)), dma((nt,)),
         dma((nt,)), dma((nt,)), dma((nt,)), dma((nt,)), dma((nt,)), dma((nt,)),
-        dma((2, 2, nt)), dma((2, 2, nt)), dma((2, 2)), dma((2, 2)), dma,
+        dma((2, 2, nt)), dma((2, 2, nt)), dma((2, 2)), dma((2, 2)), dma((2,)), dma((2,)),
     ]
-    return pl.pallas_call(
+    moved, grazed, factor = pl.pallas_call(
         functools.partial(kernel, (nt, nx, ny, t_dev, lev, t_dev * nt)),
-        out_shape=jax.ShapeDtypeStruct(tracers.shape, F32),
-        in_specs=[pl.BlockSpec(memory_space=pl.ANY)] * 8,
-        out_specs=pl.BlockSpec(memory_space=pl.ANY),
+        out_shape=(
+            jax.ShapeDtypeStruct(tracers.shape, F32),
+            jax.ShapeDtypeStruct(tracers.shape, F32),
+            jax.ShapeDtypeStruct((nt, own, *tile), F32),
+        ),
+        in_specs=[pl.BlockSpec(memory_space=pltpu.HBM)] * 8,
+        out_specs=[pl.BlockSpec(memory_space=pltpu.VMEM)] * 3,
         scratch_shapes=scratch,
-        compiler_params=pltpu.CompilerParams(collective_id=0, has_side_effects=True),
+        compiler_params=pltpu.CompilerParams(
+            collective_id=0, has_side_effects=True, vmem_limit_bytes=20 * 1024 * 1024
+        ),
         name="plankton",
-    )(tracers, fluxes, diff_east, diff_north, column_depth, grazers, groups, preference)
+    )(*[
+        pltpu.with_memory_space_constraint(a, pltpu.HBM)
+        for a in (tracers, fluxes, diff_east, diff_north, column_depth, grazers, groups, preference)
+    ])
+    return moved - factor.reshape(lev, *tile)[None] * grazed
 
 
 def solution(mesh):

time: 37.2 us -> 37.9 us (1.019)
  local copies, waits for them, and re-layouts: 2.06 us -> 0 us
  Pallas kernels: 35 us -> 36.8 us
  other arithmetic: 0 us -> 0.97 us
    unnamed x1 -> x0, local copies, waits for them, and re-layouts: 2.06 us -> none
    pallas_call x1, Pallas kernels: 35 us -> 36.8 us  [on_device(): pl.pallas_call(functools.partial(kernel, (nt, nx, ny, t_dev, lev, t_dev *...]
    sub x0 -> x1, other arithmetic: none -> 0.97 us  [on_device(): return moved - factor.reshape(lev, *tile)[None] * grazed]
where the time goes in v2:
time: 37.9 us; the launch traced here: 37.8 us
  Pallas kernels  36.8 us (97%)
  other arithmetic  0.97 us (3%)
    pallas_call x1, Pallas kernels, on_device(): pl.pallas_call(functools.partial(kernel, (nt, nx, ny, t_dev, lev, t_dev *...  36.8 us
    sub x1, other arithmetic, on_device(): return moved - factor.reshape(lev, *tile)[None] * grazed  0.97 us

profile of v2, /device:TPU:1, one launch (start us, length us, event | category | flops | bytes accessed | tf_op | source)
XLA Modules:
  0.0 37.8 jit_solution(11578917682914651164)
XLA Ops:
  0.0 36.8 %plankton.1 = (f32[12,16,8,128]{3,2,1,0:T(8,128)S(1)}, f32[12,16,8,128]{3,2,1,0:T(8,128)S(1)}, f32[8,2,8,128]{3,2,1,0:T(8,128)S(1)}) custom-call(f32[12,16,8,128]{3,2,1,0:T(8,128)} %tr.1, f32[3,2,8,128]{3,2,1,0:T(8,128)} %fl.1, f32[8,128]{1,0:T(8,128)} %de.1, f32[8,128]{1,0:T(8,128)} %dn.1, s32[8,128]{1,0:T(8,128)} %dep.1, f32[16,8,128]{2,1,0:T(8,128)} %gz.1, ...), custom_call_target="tpu_custom_call" | custom-call | tf_op jit(solution)/shard_map/plankton/pallas_call | solution.py:519
  36.8 1.0 %multiply_subtract_fusion = f32[12,16,8,128]{3,2,1,0:T(8,128)} fusion(f32[12,16,8,128]{3,2,1,0:T(8,128)S(1)} %get-tuple-element.8, f32[12,16,8,128]{3,2,1,0:T(8,128)S(1)} %get-tuple-element.10, f32[16,8,128]{2,1,0:T(8,128)S(1)} %bitcast.1), kind=kLoop, calls=%fused_computation | loop fusion | flops 393216 | bytes 2424832 | tf_op jit(solution)/shard_map/sub | solution.py:537

commit v3 on v2

--- a/solution.py
+++ b/solution.py
@@ -125,7 +125,7 @@
         pqs[j, own + b] = q_sum
         return pack_level(0, l, tiles, acc)
 
-    acc = lax.fori_loop(0, lev, first, tuple(zero for _ in range(t_dev)))
+    acc = lax.fori_loop(0, lev, first, tuple(zero for _ in range(t_dev)), unroll=4)
     for t in range(t_dev):
         yp[0, t] = acc[t]
 
@@ -292,39 +292,56 @@
 
         lax.fori_loop(0, t_dev // 2, pair, 0)
 
+    group = 4
+    steps = lev // group
+
     def y_part(s):
-        def slopes(l, slot):
-            h = hy[l]
-            h_up = roll(h, -1)
-            for t in range(t_dev):
-                c = ext[s, t, l, pl.ds(IN, 8), :]
-                jump = h * (c - roll(c, 1))
-                jump_up = h_up * (roll(c, -1) - c)
-                slope = minmod(jump, jump_up)
-                yst[slot, 0, t] = c + slope
-                yst[slot, 1, t] = c - slope
-                yst[slot, 2, t] = jump
-                yst[slot, 3, t] = jump_up
-
-        def fluxes(l, slot):
-            f, k = fy[l], ky[l]
-            f_up, k_up = roll(f, -1), roll(k, -1)
-            ahead, ahead_up = f > 0.0, f_up > 0.0
-            for t in range(t_dev):
-                fore, aft = yst[slot, 0, t], yst[slot, 1, t]
-                carried = f * jnp.where(ahead, roll(fore, 1), aft) - k * yst[slot, 2, t]
-                carried_up = f_up * jnp.where(ahead_up, fore, roll(aft, -1)) - k_up * yst[slot, 3, t]
-                outer = pltpu.roll(ge[t], (LANES - 4) - 8 * l, 1)
-                adv[t, l] = adv[t, l] + jnp.where(at_edge, outer, carried - carried_up)
-
-        def level(l, carry):
-            slopes(l, lax.rem(l, 2))
-            fluxes(l - 1, lax.rem(l + 1, 2))
+        def jumps(g):
+            for i in range(group):
+                h = hy[g * group + i]
+                for t in range(t_dev):
+                    c = ext[s, t, g * group + i, pl.ds(IN, 8), :]
+                    yst[0, i, t] = h * (c - roll(c, 1))
+
+        def slopes(g):
+            for i in range(group):
+                for t in range(t_dev):
+                    c, jump = ext[s, t, g * group + i, pl.ds(IN, 8), :], yst[0, i, t]
+                    slope = minmod(jump, roll(jump, -1))
+                    yst[1, i, t] = c + slope
+                    yst[2, i, t] = c - slope
+                    yst[3, i, t] = jump
+
+        def fluxes(g):
+            for i in range(group):
+                f, k = fy[g * group + i], ky[g * group + i]
+                ahead = f > 0.0
+                for t in range(t_dev):
+                    face = jnp.where(ahead, roll(yst[1, i, t], 1), yst[2, i, t])
+                    yst[4, i, t] = f * face - k * yst[3, i, t]
+
+        def tendencies(g):
+            for i in range(group):
+                l = g * group + i
+                for t in range(t_dev):
+                    carried = yst[4, i, t]
+                    outer = pltpu.roll(ge[t], (LANES - 4) - 8 * l, 1)
+                    adv[t, l] = adv[t, l] + jnp.where(at_edge, outer, carried - roll(carried, -1))
+
+        stages = (tendencies, fluxes, slopes, jumps)
+
+        def step(g, carry):
+            for k in range(4):
+                stages[k](g - 3 + k)
             return carry
 
-        slopes(0, 0)
-        lax.fori_loop(1, lev, level, 0)
-        fluxes(lev - 1, (lev - 1) % 2)
+        for g in range(3):
+            for m in range(g, -1, -1):
+                stages[3 - m](g - m)
+        lax.fori_loop(3, steps, step, 0)
+        for g in range(steps, steps + 3):
+            for m in range(3, g - steps, -1):
+                stages[3 - m](g - m)
 
     def x_part(s):
         def chunk(j, carry):
@@ -431,7 +448,7 @@
             tiles.append(c)
         return pack_level(1, l, tiles, acc)
 
-    acc = lax.fori_loop(0, lev, second, tuple(zero for _ in range(t_dev)))
+    acc = lax.fori_loop(0, lev, second, tuple(zero for _ in range(t_dev)), unroll=4)
     for t in range(t_dev):
         yp[1, t] = acc[t]
     for c in y_copies(1):
@@ -507,7 +524,7 @@
         v(nt, own, *tile), v(own, *tile),
         v(2, lev, 2 * t_dev, LANES), v(2, lev, 2 * t_dev, LANES),
         v(2, lev, 2 * t_dev, LANES), v(2, lev, 2 * t_dev, LANES),
-        v(2, t_dev, *tile), v(2, t_dev, *tile), v(2, t_dev, *tile), v(t_dev, *tile), v(2, 4, t_dev, *tile),
+        v(2, t_dev, *tile), v(2, t_dev, *tile), v(2, t_dev, *tile), v(t_dev, *tile), v(5, 4, t_dev, *tile),
         v(2 * lev, LANES), v(2 * lev, LANES), v(2 * lev, LANES), v(2 * lev, LANES), v(2 * t_dev // 8, *tile),
         v(lev, *tile), v(lev, *tile), v(lev, *tile), v(lev, *tile), v(lev, *tile),
         v(lev, 24, LANES), v(lev, 24, LANES), v(24, LANES), v(6, *tile),

time: 37.9 us -> 31.7 us (0.84)
  Pallas kernels: 36.8 us -> 30.6 us
    pallas_call x1, Pallas kernels: 36.8 us -> 30.6 us  [on_device(): pl.pallas_call(functools.partial(kernel, (nt, nx, ny, t_dev, lev, t_dev *...]
where the time goes in v3:
time: 31.7 us; the launch traced here: 31.6 us
  Pallas kernels  30.6 us (97%)
  other arithmetic  0.97 us (3%)
    pallas_call x1, Pallas kernels, on_device(): pl.pallas_call(functools.partial(kernel, (nt, nx, ny, t_dev, lev, t_dev *...  30.6 us
    sub x1, other arithmetic, on_device(): return moved - factor.reshape(lev, *tile)[None] * grazed  0.97 us

profile of v3, /device:TPU:1, one launch (start us, length us, event | category | flops | bytes accessed | tf_op | source)
XLA Modules:
  0.0 31.6 jit_solution(6783237481610955171)
XLA Ops:
  0.0 30.6 %plankton.1 = (f32[12,16,8,128]{3,2,1,0:T(8,128)S(1)}, f32[12,16,8,128]{3,2,1,0:T(8,128)S(1)}, f32[8,2,8,128]{3,2,1,0:T(8,128)S(1)}) custom-call(f32[12,16,8,128]{3,2,1,0:T(8,128)} %tr.1, f32[3,2,8,128]{3,2,1,0:T(8,128)} %fl.1, f32[8,128]{1,0:T(8,128)} %de.1, f32[8,128]{1,0:T(8,128)} %dn.1, s32[8,128]{1,0:T(8,128)} %dep.1, f32[16,8,128]{2,1,0:T(8,128)} %gz.1, ...), custom_call_target="tpu_custom_call" | custom-call | tf_op jit(solution)/shard_map/plankton/pallas_call | solution.py:536
  30.6 1.0 %multiply_subtract_fusion = f32[12,16,8,128]{3,2,1,0:T(8,128)} fusion(f32[12,16,8,128]{3,2,1,0:T(8,128)S(1)} %get-tuple-element.8, f32[12,16,8,128]{3,2,1,0:T(8,128)S(1)} %get-tuple-element.10, f32[16,8,128]{2,1,0:T(8,128)S(1)} %bitcast.1), kind=kLoop, calls=%fused_computation | loop fusion | flops 393216 | bytes 2424832 | tf_op jit(solution)/shard_map/sub | solution.py:554

commit v4 on v3

--- a/solution.py
+++ b/solution.py
@@ -24,32 +24,39 @@
 
 def kernel(
     dims, tr, fl, de, dn, dep, gz, grp, prf, adv, grazed, f2,
-    ext, flv, dev, dnv, depv, gzv, grps, prfs, tv,
-    cxs, cxl, cxh, cys, cyl, cyh, fa, fb, fx,
+    ext, dev, dnv, depv, gzv, grps, prfs, tv,
+    cxs, cxl, cxh, cys, cyl, cyh, fa, fxs, fxl, fes, fel, fx,
     pqs, pqr, rs, rr, f1, own1,
     sxl, sxh, xl, xh, yp, yl, yr, ge, yst, gsl, gsh, gxl, gxh, tx,
     hy, fy, ky, hz, fz, hx, kx, wx, ec,
-    lsem, csem, crec, fas, far, fbs, fbr, pqss, pqrs, rss, rrs, f1s, f1r, f2s, f2r,
+    lsem, csem, crec, fas, far, pqss, pqrs, rss, rrs, f1s, f1r, f2s, f2r,
     xss, xrs, yss, yrs, gss, grs,
 ):
     nt, nx, ny, t_dev, lev, total = dims
     own = lev // nt
     me, gx, gy = lax.axis_index("tracer"), lax.axis_index("gx"), lax.axis_index("gy")
-    left, right = lax.rem(gy + ny - 1, ny), lax.rem(gy + 1, ny)
+    left, right = gy - 1, gy + 1
+    has_left, has_right = gy > 0, gy < ny - 1
     has_lo, has_hi = gx > 0, gx < nx - 1
     others = [lax.rem(me + d, nt) for d in range(1, nt)]
 
-    loads = [
-        (tr, ext.at[0, :, :, pl.ds(IN, 8), :]), (fl, flv), (de, dev), (dn, dnv), (dep, depv),
-        (gz, gzv), (grp, grps), (prf, prfs),
-    ]
+    loads = [(fl, fa.at[me]), (de, dev), (dn, dnv), (dep, depv), (grp, grps), (prf, prfs), (gz, gzv)]
+    for j in range(nt):
+        c = pl.ds(j * own, own)
+        loads.append((tr.at[:, c], ext.at[0, :, c, pl.ds(IN, 8), :]))
     loads = [pltpu.make_async_copy(a, b, lsem.at[i]) for i, (a, b) in enumerate(loads)]
 
     barrier = pltpu.get_barrier_semaphore()
     for peer in others:
         pl.semaphore_signal(barrier, inc=1, device_id={"tracer": peer}, device_id_type=MESH)
-    for z in (left, right):
-        pl.semaphore_signal(barrier, inc=1, device_id={"gy": z}, device_id_type=MESH)
+
+    @pl.when(has_left)
+    def _():
+        pl.semaphore_signal(barrier, inc=1, device_id={"gy": left}, device_id_type=MESH)
+
+    @pl.when(has_right)
+    def _():
+        pl.semaphore_signal(barrier, inc=1, device_id={"gy": right}, device_id_type=MESH)
 
     @pl.when(has_lo)
     def _():
@@ -74,7 +81,21 @@
             base = base + roll(base, s)
         return base
 
-    for c in loads[1:]:
+    def send(src, dst, ssem, rsem, to):
+        return pltpu.make_async_remote_copy(
+            src_ref=src, dst_ref=dst, send_sem=ssem, recv_sem=rsem, device_id=to, device_id_type=MESH
+        )
+
+    fa_out = [
+        send(fl, fa.at[me], fas.at[d], far.at[me], {"tracer": peer}) for d, peer in enumerate(others)
+    ]
+
+    near = [has_lo, has_hi, has_left, has_right]
+    pl.semaphore_wait(barrier, nt - 1 + sum(h.astype(jnp.int32) for h in near))
+    for c in fa_out:
+        c.start()
+
+    for c in loads[:6]:
         c.wait()
     for t in range(t_dev):
         w = jnp.full((8, LANES), prfs[grps[t]], F32)
@@ -83,60 +104,14 @@
     depth = depv[...].astype(F32)
     cxs[0] = depth
     cxs[1] = dev[...]
-    rows_tile = zero
-    lanes_tile = zero
-    for b in range(own):
-        rows_tile = jnp.where(row == b, flv[0, b, pl.ds(7, 1), :], rows_tile)
-        lanes_tile = jnp.where(plev == me * own + b, spread(flv[1, b]), lanes_tile)
-    cxs[2] = rows_tile
     cys[0] = spread(depth)
     cys[1] = spread(dnv[...])
-    cys[2] = lanes_tile
-    for k in range(3):
-        for b in range(own):
-            fa[me, k * own + b] = flv[k, b]
-    fa[me, 3 * own] = lanes_tile
-    loads[0].wait()
-
-    def send(src, dst, ssem, rsem, to):
-        return pltpu.make_async_remote_copy(
-            src_ref=src, dst_ref=dst, send_sem=ssem, recv_sem=rsem, device_id=to, device_id_type=MESH
-        )
-
-    def pack_level(s, l, tiles, acc):
-        acc = list(acc)
-        for t in range(t_dev):
-            if s == 0:
-                sxl[s, l, pl.ds(2 * t, 2), :] = ext[s, t, l, pl.ds(IN, 2), :]
-                sxh[s, l, pl.ds(2 * t, 2), :] = ext[s, t, l, pl.ds(IN + 6, 2), :]
-            acc[t] = jnp.where(plev == l, pltpu.roll(tiles[t], 8 * l + 4, 1), acc[t])
-        return tuple(acc)
-
-    def first(l, acc):
-        tiles = [ext[0, t, l, pl.ds(IN, 8), :] for t in range(t_dev)]
-        p_sum, q_sum = zero, zero
-        for t in range(t_dev):
-            w = tv[t]
-            wc = w * tiles[t]
-            p_sum = p_sum + wc
-            q_sum = q_sum + w * wc
-        j, b = l // own, lax.rem(l, own)
-        pqs[j, b] = p_sum
-        pqs[j, own + b] = q_sum
-        return pack_level(0, l, tiles, acc)
-
-    acc = lax.fori_loop(0, lev, first, tuple(zero for _ in range(t_dev)), unroll=4)
-    for t in range(t_dev):
-        yp[0, t] = acc[t]
-
-    pl.semaphore_wait(barrier, nt - 1 + 2 + has_lo.astype(jnp.int32) + has_hi.astype(jnp.int32))
-
     c_right = send(cys, cyl, csem.at[0], crec.at[0], {"gy": right})
     c_left = send(cys.at[pl.ds(0, 1)], cyh, csem.at[1], crec.at[1], {"gy": left})
     c_up = send(cxs, cxl, csem.at[2], crec.at[2], {"gx": gx + 1})
     c_down = send(cxs.at[pl.ds(0, 1)], cxh, csem.at[3], crec.at[3], {"gx": gx - 1})
-    c_right.start()
-    c_left.start()
+    pl.when(has_right)(c_right.start)
+    pl.when(has_left)(c_left.start)
     pl.when(has_hi)(c_up.start)
     pl.when(has_lo)(c_down.start)
 
@@ -145,6 +120,11 @@
             send(yp.at[s], yl.at[s], yss.at[s, 0], yrs.at[s, 0], {"gy": right}),
             send(yp.at[s], yr.at[s], yss.at[s, 1], yrs.at[s, 1], {"gy": left}),
         )
+
+    def y_start(s):
+        to_right, to_left = y_copies(s)
+        pl.when(has_right)(to_right.start)
+        pl.when(has_left)(to_left.start)
 
     def x_copies(s, j):
         c = pl.ds(j * own, own)
@@ -172,22 +152,56 @@
         for peer in others:
             send(src.at[peer], dst.at[peer], ssem.at[peer], rsem.at[peer], {"tracer": peer}).wait_recv()
 
-    for peer in others:
-        scatter(pqs, pqr, pqss, pqrs, peer).start()
-    gather_start(fa, fas, far)
-    for c in y_copies(0):
-        c.start()
-
     def x_start(s, j):
         up, down = x_copies(s, j)
         pl.when(has_hi)(up.start)
         pl.when(has_lo)(down.start)
 
     for j in range(nt):
+        loads[7 + j].wait()
+        for b in range(own):
+            l = j * own + b
+            p_sum, q_sum = zero, zero
+            for t in range(t_dev):
+                two, tile = pl.ds(2 * t, 2), ext[0, t, l, pl.ds(IN, 8), :]
+                sxl[0, l, two, :] = ext[0, t, l, pl.ds(IN, 2), :]
+                sxh[0, l, two, :] = ext[0, t, l, pl.ds(IN + 6, 2), :]
+                w = tv[t]
+                wc = w * tile
+                p_sum = p_sum + wc
+                q_sum = q_sum + w * wc
+            pqs[j, b] = p_sum
+            pqs[j, own + b] = q_sum
         x_start(0, j)
 
-    c_right.wait_recv()
-    c_left.wait_recv()
+        @pl.when(j != me)
+        def _():
+            scatter(pqs, pqr, pqss, pqrs, j).start()
+
+
+    def pack_level(s, l, acc):
+        tiles = [ext[s, t, l, pl.ds(IN, 8), :] for t in range(t_dev)]
+        return tuple(
+            jnp.where(plev == l, pltpu.roll(tiles[t], 8 * l + 4, 1), acc[t]) for t in range(t_dev)
+        )
+
+    blank = tuple(zero for _ in range(t_dev))
+    acc = lax.fori_loop(0, lev, lambda l, acc: pack_level(0, l, acc), blank, unroll=4)
+    for t in range(t_dev):
+        yp[0, t] = acc[t]
+    y_start(0)
+
+    dn_low = 2.0 * roll(dnv[...], 1)
+    depth_y = jnp.minimum(depth, roll(depth, 1))
+    for l in range(lev):
+        open_y = (depth_y > l).astype(F32)
+        hy[l] = 0.5 * open_y
+        ky[l] = dn_low * open_y
+        if l:
+            hz[l] = 0.5 * (depth > l).astype(F32)
+
+    pl.when(has_left)(c_right.wait_recv)
+    pl.when(has_right)(c_left.wait_recv)
     pl.when(has_hi)(c_down.wait_recv)
 
     @pl.when(has_lo)
@@ -196,19 +210,26 @@
 
     @pl.when(gx == 0)
     def _():
-        for k in range(3):
+        for k in range(2):
             cxl[k] = zero
 
     @pl.when(gx == nx - 1)
     def _():
         cxh[0] = zero
 
-    fb[me, 0] = cxl[2]
-    fb[me, 1] = cyl[2]
-    gather_start(fb, fbs, fbr)
-
-    dep_l = cyl[0] * (gy > 0).astype(F32)
-    dep_r = cyh[0] * (gy < ny - 1).astype(F32)
+    @pl.when(gy == 0)
+    def _():
+        for k in range(2):
+            cyl[k] = zero
+        fel[...] = zero
+        yl[...] = jnp.zeros_like(yl)
+
+    @pl.when(gy == ny - 1)
+    def _():
+        cyh[0] = zero
+        yr[...] = jnp.zeros_like(yr)
+
+    dep_l, dep_r = cyl[0], cyh[0]
     dep_m = cys[0]
     plevf = plev.astype(F32)
     wet0 = (plevf < jnp.where(e < 4, dep_l, dep_m)).astype(F32)
@@ -219,44 +240,41 @@
     wx[pl.ds(LO, 2), :] = cxl[0, pl.ds(6, 2), :]
     wx[pl.ds(IN, 8), :] = depth
     wx[pl.ds(HI, 2), :] = cxh[0, pl.ds(0, 2), :]
-    for k in range(2 * own):
-        pqr[me, k] = pqs[me, k]
-    scatter_wait(pqs, pqr, pqss, pqrs)
-    scale = 4.0 / total
-    for b in range(own):
-        prey = pqr[0, b]
-        sq = pqr[0, own + b]
-        for j in range(1, nt):
-            prey = prey + pqr[j, b]
-            sq = sq + pqr[j, own + b]
-        f1[me, b] = gzv[me * own + b] / (1.0 + scale * prey)
-        own1[b] = sq
-    gather_start(f1, f1s, f1r)
-
-    gather_wait(fa, fas, far)
-    flux_edge = fa[0, 3 * own]
-    for j in range(1, nt):
-        flux_edge = flux_edge + fa[j, 3 * own]
+    d_low = jnp.concatenate([2.0 * cxl[1, pl.ds(7, 1), :], 2.0 * dev[pl.ds(0, 7), :]], axis=0)
+    d_up = 2.0 * dev[...]
+    depth_x = [
+        jnp.minimum(wx[pl.ds(LO + k, 8), :], wx[pl.ds(LO + 1 + k, 8), :]) for k in range(4)
+    ]
+    for l in range(lev):
+        opens = [(depth_x[k] > l).astype(F32) for k in range(4)]
+        hx[l, pl.ds(IN - 1, 8), :] = 0.5 * opens[0]
+        hx[l, pl.ds(IN + 2, 8), :] = 0.5 * opens[3]
+        kx[l, pl.ds(IN, 8), :] = d_low * opens[1]
+        kx[l, pl.ds(IN + 1, 8), :] = d_up * opens[2]
+    for peer in others:
+        send(fl, fa.at[peer], fas.at[0], far.at[peer], {"tracer": peer}).wait_recv()
+    flux_edge = zero
+    for l in range(lev):
+        j, b = l // own, l % own
+        flux_edge = jnp.where(plev == l, roll(fa[j, 1, b], 8 * l + 4), flux_edge)
+        fxs[pl.ds(l, 1), :] = fa[j, 0, b, pl.ds(7, 1), :]
+    fes[...] = flux_edge
+    f_right = send(fes, fel, csem.at[4], crec.at[4], {"gy": right})
+    f_up = send(fxs, fxl, csem.at[5], crec.at[5], {"gx": gx + 1})
+    pl.when(has_right)(f_right.start)
+    pl.when(has_hi)(f_up.start)
     ec[0] = 0.5 * open0
     ec[1] = flux_edge
     ec[2] = 2.0 * open0 * roll(jnp.where(e < 4, cyl[1], cys[1]), 1)
     ec[3] = 0.5 * open1
     ec[4] = roll(flux_edge, 1) * open1
     ec[5] = 2.0 * open1 * roll(cys[1], 1)
-    dn_low = 2.0 * roll(dnv[...], 1)
-    depth_y = jnp.minimum(depth, roll(depth, 1))
-
     for l in range(lev):
         j, b = l // own, l % own
-        open_y = (depth_y > l).astype(F32)
-        hy[l] = 0.5 * open_y
-        fy[l] = roll(fa[j, own + b], 1) * open_y
-        ky[l] = dn_low * open_y
+        fy[l] = roll(fa[j, 1, b], 1) * (depth_y > l).astype(F32)
         if l:
-            open_z = (depth > l).astype(F32)
-            hz[l] = 0.5 * open_z
-            fz[l] = fa[(l - 1) // own, 2 * own + (l - 1) % own] * open_z
-        fx[l, pl.ds(IN, 8), :] = fa[j, b]
+            fz[l] = fa[(l - 1) // own, 2, (l - 1) % own] * (depth > l).astype(F32)
+        fx[l, pl.ds(IN, 8), :] = fa[j, 0, b]
 
     def edge(cells, h, flux, kappa):
         below = roll(cells, 1)
@@ -266,8 +284,9 @@
         return carried - roll(carried, -1)
 
     def y_edges(s):
-        for c in y_copies(s):
-            c.wait_recv()
+        from_left, from_right = y_copies(s)
+        pl.when(has_left)(from_left.wait_recv)
+        pl.when(has_right)(from_right.wait_recv)
         for t in range(t_dev):
             mine = yp[s, t]
             low = edge(jnp.where(e < 4, yl[s, t], mine), ec[0], ec[1], ec[2])
@@ -401,32 +420,40 @@
         def _():
             xh[s] = jnp.zeros_like(xh[s])
 
-    gather_wait(fb, fbs, fbr)
-    flux_edge = fb[0, 1]
-    for j in range(1, nt):
-        flux_edge = flux_edge + fb[j, 1]
-    ec[1] = roll(jnp.where(e < 4, flux_edge, ec[1]), 1) * open0
+    z_part(0)
+    loads[6].wait()
+    for k in range(2 * own):
+        pqr[me, k] = pqs[me, k]
+    scatter_wait(pqs, pqr, pqss, pqrs)
+    scale = 4.0 / total
+    for b in range(own):
+        prey = pqr[0, b]
+        sq = pqr[0, own + b]
+        for j in range(1, nt):
+            prey = prey + pqr[j, b]
+            sq = sq + pqr[j, own + b]
+        f1[me, b] = gzv[me * own + b] / (1.0 + scale * prey)
+        own1[b] = sq
+    gather_start(f1, f1s, f1r)
+
+    pl.when(has_left)(f_right.wait_recv)
+    ec[1] = roll(jnp.where(e < 4, fel[...], ec[1]), 1) * open0
+    y_edges(0)
+    y_part(0)
+    pl.when(has_lo)(f_up.wait_recv)
+
+    @pl.when(gx == 0)
+    def _():
+        fxl[...] = jnp.zeros_like(fxl)
+
     for l in range(lev):
-        fx[l, pl.ds(IN - 1, 1), :] = fb[l // own, 0, pl.ds(l % own, 1), :]
-    d_low = jnp.concatenate([2.0 * cxl[1, pl.ds(7, 1), :], 2.0 * dev[pl.ds(0, 7), :]], axis=0)
-    d_up = 2.0 * dev[...]
-    depth_x = [
-        jnp.minimum(wx[pl.ds(LO + k, 8), :], wx[pl.ds(LO + 1 + k, 8), :]) for k in range(4)
-    ]
+        fx[l, pl.ds(IN - 1, 1), :] = fxl[pl.ds(l, 1), :]
     for l in range(lev):
-        opens = [(depth_x[k] > l).astype(F32) for k in range(4)]
-        low = fx[l, pl.ds(IN - 1, 8), :] * opens[1]
-        up = fx[l, pl.ds(IN, 8), :] * opens[2]
-        hx[l, pl.ds(IN - 1, 8), :] = 0.5 * opens[0]
-        hx[l, pl.ds(IN + 2, 8), :] = 0.5 * opens[3]
+        low = fx[l, pl.ds(IN - 1, 8), :] * (depth_x[1] > l).astype(F32)
+        up = fx[l, pl.ds(IN, 8), :] * (depth_x[2] > l).astype(F32)
         fx[l, pl.ds(IN - 1, 8), :] = low
         fx[l, pl.ds(IN, 8), :] = up
-        kx[l, pl.ds(IN, 8), :] = d_low * opens[1]
-        kx[l, pl.ds(IN + 1, 8), :] = d_up * opens[2]
-
-    z_part(0)
-    y_edges(0)
-    y_part(0)
+
     x_part(0)
     gather_wait(f1, f1s, f1r)
     for l in range(lev):
@@ -438,21 +465,20 @@
     pl.when(has_lo)(g_down.start)
 
     def second(l, acc):
+        acc = list(acc)
         j, b = l // own, lax.rem(l, own)
         factor = f1[j, b]
-        tiles = []
         for t in range(t_dev):
             c = adv[t, l] - (tv[t] * factor) * ext[0, t, l, pl.ds(IN, 8), :]
             ext[1, t, l, pl.ds(IN, 8), :] = c
             grazed[t, l] = tv[t] * c
-            tiles.append(c)
-        return pack_level(1, l, tiles, acc)
-
-    acc = lax.fori_loop(0, lev, second, tuple(zero for _ in range(t_dev)), unroll=4)
+            acc[t] = jnp.where(plev == l, pltpu.roll(c, 8 * l + 4, 1), acc[t])
+        return tuple(acc)
+
+    acc = lax.fori_loop(0, lev, second, blank, unroll=4)
     for t in range(t_dev):
         yp[1, t] = acc[t]
-    for c in y_copies(1):
-        c.start()
+    y_start(1)
     z_part(1)
 
     for b in range(own):
@@ -482,21 +508,24 @@
     x_part(1)
     gather_wait(f2, f2s, f2r)
 
-    c_right.wait_send()
-    c_left.wait_send()
+    pl.when(has_right)(c_right.wait_send)
+    pl.when(has_left)(c_left.wait_send)
     pl.when(has_hi)(c_up.wait_send)
     pl.when(has_lo)(c_down.wait_send)
     pl.when(has_hi)(g_up.wait_send)
     pl.when(has_lo)(g_down.wait_send)
     for s in range(STEPS):
-        for c in y_copies(s):
-            c.wait_send()
+        to_right, to_left = y_copies(s)
+        pl.when(has_right)(to_right.wait_send)
+        pl.when(has_left)(to_left.wait_send)
         for j in range(nt):
             up, down = x_copies(s, j)
             pl.when(has_hi)(up.wait_send)
             pl.when(has_lo)(down.wait_send)
-    gather_done(fa, fas, far)
-    gather_done(fb, fbs, fbr)
+    for c in fa_out:
+        c.wait_send()
+    pl.when(has_right)(f_right.wait_send)
+    pl.when(has_hi)(f_up.wait_send)
     gather_done(f1, f1s, f1r)
     gather_done(f2, f2s, f2r)
     for peer in others:
@@ -516,10 +545,10 @@
 
     scratch = [
         v(2, t_dev, lev, 24, LANES),
-        v(3, own, *tile), v(*tile), v(*tile), pltpu.VMEM(tile, jnp.int32), v(lev, *tile),
+        v(*tile), v(*tile), pltpu.VMEM(tile, jnp.int32), v(lev, *tile),
         pltpu.SMEM(groups.shape, jnp.int32), pltpu.SMEM(preference.shape, F32), v(t_dev, *tile),
-        v(3, *tile), v(3, *tile), v(1, *tile), v(3, *tile), v(3, *tile), v(1, *tile),
-        v(nt, 3 * own + 1, *tile), v(nt, 2, *tile), v(lev, 24, LANES),
+        v(2, *tile), v(2, *tile), v(1, *tile), v(2, *tile), v(2, *tile), v(1, *tile),
+        v(nt, 3, own, *tile), v(lev, LANES), v(lev, LANES), v(*tile), v(*tile), v(lev, 24, LANES),
         v(nt, 2 * own, *tile), v(nt, 2 * own, *tile), v(nt, own, *tile), v(nt, own, *tile),
         v(nt, own, *tile), v(own, *tile),
         v(2, lev, 2 * t_dev, LANES), v(2, lev, 2 * t_dev, LANES),
@@ -528,8 +557,8 @@
         v(2 * lev, LANES), v(2 * lev, LANES), v(2 * lev, LANES), v(2 * lev, LANES), v(2 * t_dev // 8, *tile),
         v(lev, *tile), v(lev, *tile), v(lev, *tile), v(lev, *tile), v(lev, *tile),
         v(lev, 24, LANES), v(lev, 24, LANES), v(24, LANES), v(6, *tile),
-        dma((8,)), dma((4,)), dma((4,)),
-        dma((nt,)), dma((nt,)), dma((nt,)), dma((nt,)), dma((nt,)), dma((nt,)),
+        dma((7 + nt,)), dma((6,)), dma((6,)),
+        dma((nt,)), dma((nt,)), dma((nt,)), dma((nt,)),
         dma((nt,)), dma((nt,)), dma((nt,)), dma((nt,)), dma((nt,)), dma((nt,)),
         dma((2, 2, nt)), dma((2, 2, nt)), dma((2, 2)), dma((2, 2)), dma((2,)), dma((2,)),
     ]

time: 31.7 us -> 27.7 us (0.87)
  the two profiles are of different devices: /device:TPU:1 before, /device:TPU:100 now
where the time goes in v4:
time: 27.7 us; the launch traced here: 27.6 us
  Pallas kernels  26.6 us (96%)
  other arithmetic  0.97 us (4%)
    pallas_call x1, Pallas kernels, on_device(): pl.pallas_call(functools.partial(kernel, (nt, nx, ny, t_dev, lev, t_dev *...  26.6 us
    sub x1, other arithmetic, on_device(): return moved - factor.reshape(lev, *tile)[None] * grazed  0.97 us

profile of v4, /device:TPU:100, one launch (start us, length us, event | category | flops | bytes accessed | tf_op | source)
XLA Modules:
  0.0 27.6 jit_solution(906366157568613831)
XLA Ops:
  0.0 26.6 %plankton.1 = (f32[12,16,8,128]{3,2,1,0:T(8,128)S(1)}, f32[12,16,8,128]{3,2,1,0:T(8,128)S(1)}, f32[8,2,8,128]{3,2,1,0:T(8,128)S(1)}) custom-call(f32[12,16,8,128]{3,2,1,0:T(8,128)} %tr.1, f32[3,2,8,128]{3,2,1,0:T(8,128)} %fl.1, f32[8,128]{1,0:T(8,128)} %de.1, f32[8,128]{1,0:T(8,128)} %dn.1, s32[8,128]{1,0:T(8,128)} %dep.1, f32[16,8,128]{2,1,0:T(8,128)} %gz.1, ...), custom_call_target="tpu_custom_call" | custom-call | tf_op jit(solution)/shard_map/plankton/pallas_call | solution.py:565
  26.6 1.0 %multiply_subtract_fusion = f32[12,16,8,128]{3,2,1,0:T(8,128)} fusion(f32[12,16,8,128]{3,2,1,0:T(8,128)S(1)} %get-tuple-element.8, f32[12,16,8,128]{3,2,1,0:T(8,128)S(1)} %get-tuple-element.10, f32[16,8,128]{2,1,0:T(8,128)S(1)} %bitcast.1), kind=kLoop, calls=%fused_computation | loop fusion | flops 393216 | bytes 2424832 | tf_op jit(solution)/shard_map/sub | solution.py:583

commit v5 on v4

--- a/solution.py
+++ b/solution.py
@@ -263,6 +263,22 @@
     f_up = send(fxs, fxl, csem.at[5], crec.at[5], {"gx": gx + 1})
     pl.when(has_right)(f_right.start)
     pl.when(has_hi)(f_up.start)
+
+    loads[6].wait()
+    for k in range(2 * own):
+        pqr[me, k] = pqs[me, k]
+    scatter_wait(pqs, pqr, pqss, pqrs)
+    scale = 4.0 / total
+    for b in range(own):
+        prey = pqr[0, b]
+        sq = pqr[0, own + b]
+        for j in range(1, nt):
+            prey = prey + pqr[j, b]
+            sq = sq + pqr[j, own + b]
+        f1[me, b] = gzv[me * own + b] / (1.0 + scale * prey)
+        own1[b] = sq
+    gather_start(f1, f1s, f1r)
+
     ec[0] = 0.5 * open0
     ec[1] = flux_edge
     ec[2] = 2.0 * open0 * roll(jnp.where(e < 4, cyl[1], cys[1]), 1)
@@ -344,7 +360,7 @@
                 l = g * group + i
                 for t in range(t_dev):
                     carried = yst[4, i, t]
-                    outer = pltpu.roll(ge[t], (LANES - 4) - 8 * l, 1)
+                    outer = zero if s else pltpu.roll(ge[t], (LANES - 4) - 8 * l, 1)
                     adv[t, l] = adv[t, l] + jnp.where(at_edge, outer, carried - roll(carried, -1))
 
         stages = (tendencies, fluxes, slopes, jumps)
@@ -361,6 +377,12 @@
         for g in range(steps, steps + 3):
             for m in range(3, g - steps, -1):
                 stages[3 - m](g - m)
+
+    def y_outer(l, carry):
+        for t in range(t_dev):
+            outer = pltpu.roll(ge[t], (LANES - 4) - 8 * l, 1)
+            adv[t, l] = adv[t, l] + jnp.where(at_edge, outer, zero)
+        return carry
 
     def x_part(s):
         def chunk(j, carry):
@@ -421,21 +443,6 @@
             xh[s] = jnp.zeros_like(xh[s])
 
     z_part(0)
-    loads[6].wait()
-    for k in range(2 * own):
-        pqr[me, k] = pqs[me, k]
-    scatter_wait(pqs, pqr, pqss, pqrs)
-    scale = 4.0 / total
-    for b in range(own):
-        prey = pqr[0, b]
-        sq = pqr[0, own + b]
-        for j in range(1, nt):
-            prey = prey + pqr[j, b]
-            sq = sq + pqr[j, own + b]
-        f1[me, b] = gzv[me * own + b] / (1.0 + scale * prey)
-        own1[b] = sq
-    gather_start(f1, f1s, f1r)
-
     pl.when(has_left)(f_right.wait_recv)
     ec[1] = roll(jnp.where(e < 4, fel[...], ec[1]), 1) * open0
     y_edges(0)
@@ -480,6 +487,7 @@
         yp[1, t] = acc[t]
     y_start(1)
     z_part(1)
+    y_part(1)
 
     for b in range(own):
         rr[me, b] = rs[me, b]
@@ -492,8 +500,6 @@
         f2[me, b] = gzv[me * own + b] / (1.0 + scale * prey)
     gather_start(f2, f2s, f2r)
 
-    y_edges(1)
-    y_part(1)
     pl.when(has_lo)(g_up.wait_recv)
     pl.when(has_hi)(g_down.wait_recv)
 
@@ -506,6 +512,8 @@
         gxh[...] = jnp.zeros_like(gxh)
 
     x_part(1)
+    y_edges(1)
+    lax.fori_loop(0, lev, y_outer, 0, unroll=4)
     gather_wait(f2, f2s, f2r)
 
     pl.when(has_right)(c_right.wait_send)

time: 27.7 us -> 26.9 us (0.971)
  the two profiles are of different devices: /device:TPU:100 before, /device:TPU:1 now
where the time goes in v5:
time: 26.9 us
  Pallas kernels  25.9 us (96%)
  other arithmetic  0.97 us (4%)
    pallas_call x1, Pallas kernels, on_device(): pl.pallas_call(functools.partial(kernel, (nt, nx, ny, t_dev, lev, t_dev *...  25.9 us
    sub x1, other arithmetic, on_device(): return moved - factor.reshape(lev, *tile)[None] * grazed  0.97 us

profile of v5, /device:TPU:1, one launch (start us, length us, event | category | flops | bytes accessed | tf_op | source)
XLA Modules:
  0.0 26.9 jit_solution(2730244313540640612)
XLA Ops:
  0.0 25.9 %plankton.1 = (f32[12,16,8,128]{3,2,1,0:T(8,128)S(1)}, f32[12,16,8,128]{3,2,1,0:T(8,128)S(1)}, f32[8,2,8,128]{3,2,1,0:T(8,128)S(1)}) custom-call(f32[12,16,8,128]{3,2,1,0:T(8,128)} %tr.1, f32[3,2,8,128]{3,2,1,0:T(8,128)} %fl.1, f32[8,128]{1,0:T(8,128)} %de.1, f32[8,128]{1,0:T(8,128)} %dn.1, s32[8,128]{1,0:T(8,128)} %dep.1, f32[16,8,128]{2,1,0:T(8,128)} %gz.1, ...), custom_call_target="tpu_custom_call" | custom-call | tf_op jit(solution)/shard_map/plankton/pallas_call | solution.py:573
  25.9 1.0 %multiply_subtract_fusion = f32[12,16,8,128]{3,2,1,0:T(8,128)} fusion(f32[12,16,8,128]{3,2,1,0:T(8,128)S(1)} %get-tuple-element.8, f32[12,16,8,128]{3,2,1,0:T(8,128)S(1)} %get-tuple-element.10, f32[16,8,128]{2,1,0:T(8,128)S(1)} %bitcast.1), kind=kLoop, calls=%fused_computation | loop fusion | flops 393216 | bytes 2424832 | tf_op jit(solution)/shard_map/sub | solution.py:591

commit v6 on v5

--- a/solution.py
+++ b/solution.py
@@ -104,14 +104,10 @@
     depth = depv[...].astype(F32)
     cxs[0] = depth
     cxs[1] = dev[...]
-    cys[0] = spread(depth)
-    cys[1] = spread(dnv[...])
     c_right = send(cys, cyl, csem.at[0], crec.at[0], {"gy": right})
     c_left = send(cys.at[pl.ds(0, 1)], cyh, csem.at[1], crec.at[1], {"gy": left})
     c_up = send(cxs, cxl, csem.at[2], crec.at[2], {"gx": gx + 1})
     c_down = send(cxs.at[pl.ds(0, 1)], cxh, csem.at[3], crec.at[3], {"gx": gx - 1})
-    pl.when(has_right)(c_right.start)
-    pl.when(has_left)(c_left.start)
     pl.when(has_hi)(c_up.start)
     pl.when(has_lo)(c_down.start)
 
@@ -178,6 +174,11 @@
         def _():
             scatter(pqs, pqr, pqss, pqrs, j).start()
 
+
+    cys[0] = spread(depth)
+    cys[1] = spread(dnv[...])
+    pl.when(has_right)(c_right.start)
+    pl.when(has_left)(c_left.start)
 
     def pack_level(s, l, acc):
         tiles = [ext[s, t, l, pl.ds(IN, 8), :] for t in range(t_dev)]
@@ -482,7 +483,7 @@
             acc[t] = jnp.where(plev == l, pltpu.roll(c, 8 * l + 4, 1), acc[t])
         return tuple(acc)
 
-    acc = lax.fori_loop(0, lev, second, blank, unroll=4)
+    acc = lax.fori_loop(0, lev, second, blank, unroll=8)
     for t in range(t_dev):
         yp[1, t] = acc[t]
     y_start(1)
@@ -513,7 +514,7 @@
 
     x_part(1)
     y_edges(1)
-    lax.fori_loop(0, lev, y_outer, 0, unroll=4)
+    lax.fori_loop(0, lev, y_outer, 0, unroll=8)
     gather_wait(f2, f2s, f2r)
 
     pl.when(has_right)(c_right.wait_send)

time: 26.9 us -> 26.8 us (level)
  no operation moved by 1% of the time
where the time goes in v6:
time: 26.8 us; the launch traced here: 26.7 us
  Pallas kernels  25.8 us (96%)
  other arithmetic  0.97 us (4%)
    pallas_call x1, Pallas kernels, on_device(): pl.pallas_call(functools.partial(kernel, (nt, nx, ny, t_dev, lev, t_dev *...  25.8 us
    sub x1, other arithmetic, on_device(): return moved - factor.reshape(lev, *tile)[None] * grazed  0.97 us

profile of v6, /device:TPU:1, one launch (start us, length us, event | category | flops | bytes accessed | tf_op | source)
XLA Modules:
  0.0 26.7 jit_solution(17394385448590358623)
XLA Ops:
  0.0 25.8 %plankton.1 = (f32[12,16,8,128]{3,2,1,0:T(8,128)S(1)}, f32[12,16,8,128]{3,2,1,0:T(8,128)S(1)}, f32[8,2,8,128]{3,2,1,0:T(8,128)S(1)}) custom-call(f32[12,16,8,128]{3,2,1,0:T(8,128)} %tr.1, f32[3,2,8,128]{3,2,1,0:T(8,128)} %fl.1, f32[8,128]{1,0:T(8,128)} %de.1, f32[8,128]{1,0:T(8,128)} %dn.1, s32[8,128]{1,0:T(8,128)} %dep.1, f32[16,8,128]{2,1,0:T(8,128)} %gz.1, ...), custom_call_target="tpu_custom_call" | custom-call | tf_op jit(solution)/shard_map/plankton/pallas_call | solution.py:574
  25.8 1.0 %multiply_subtract_fusion = f32[12,16,8,128]{3,2,1,0:T(8,128)} fusion(f32[12,16,8,128]{3,2,1,0:T(8,128)S(1)} %get-tuple-element.8, f32[12,16,8,128]{3,2,1,0:T(8,128)S(1)} %get-tuple-element.10, f32[16,8,128]{2,1,0:T(8,128)S(1)} %bitcast.1), kind=kLoop, calls=%fused_computation | loop fusion | flops 393216 | bytes 2424832 | tf_op jit(solution)/shard_map/sub | solution.py:592
